TPU v7x, 256 devices: a whole 4x4x8 slice. The times are simulated.
256 devices in a mesh: grp: 32 (over x, y, core), blk: 8 (over z).
Axes of the slice: x: 4, y: 4, z: 8, core: 2. Of those that a mesh axis runs over, the one named last changes fastest.
Arguments:
- tiles_near: bfloat16 [16384, 256, 256], P(('grp', 'blk')), may hold values from -0.078125 to 0.078125
- near_cols: int32 [256, 64], P(('grp', 'blk')), may hold values from 0 to 3
- tiles_far: bfloat16 [6144, 256, 256], P(('grp', 'blk')), may hold values from -0.078125 to 0.078125
- far_groups: int32 [256, 24], P(('grp', 'blk')), may hold values from 0 to 31, as said below
- need_blocks: int32 [256, 32], P(('grp', 'blk')), may hold values from -1 to 3, as said below
- start_vectors: bfloat16 [262144, 128], P(('grp', 'blk')), may hold values from -6 to 6
Outputs:
- vectors: float32 [262144, 128], P(('grp', 'blk'))
Inputs may be any that keep to these rules, and one draw needn't show every extreme that they name: need_blocks[d, h] is -1 for d's own group and for groups d reads nothing from, else a row block index below 4 of the device of group h at d's position along blk; every device reads from at least one other group. far_groups[d, t] is a group h with need_blocks[d, h] >= 0.
All inputs are finite; a program needn't handle non-finite values.
Results may differ from a plain program's by a relative error of at most 0.0029.
Values may be sent and summed in bfloat16 or wider, within the bound.
A program may use at most 128 MiB of HBM per device.

v0:
```python
import jax
import jax.numpy as jnp
from jax import lax
from jax.sharding import PartitionSpec as P

ITERS = 2


def per_device(tiles_near, near_cols, tiles_far, far_groups, need_blocks, start_vectors):
    tile_size = tiles_near.shape[1]
    vec_width = start_vectors.shape[1]
    blocks = start_vectors.shape[0] // tile_size
    group_size = lax.axis_size("blk")
    group_count = lax.axis_size("grp")
    per_source = tiles_near.shape[0] // (blocks * group_size)
    far_each = tiles_far.shape[0] // blocks
    near_tiles = tiles_near.reshape(blocks, group_size, per_source, tile_size, tile_size)
    near_index = near_cols.reshape(blocks, group_size, per_source)
    far_tiles = tiles_far.reshape(blocks, far_each, tile_size, tile_size)
    far_index = far_groups.reshape(blocks, far_each)
    wanted = need_blocks.reshape(group_count)
    total_rows = blocks * tile_size * group_size * group_count
    current = start_vectors
    vectors = start_vectors.astype(jnp.float32)
    for iteration in range(ITERS):
        local_rows = current.reshape(blocks, tile_size, vec_width)
        group_table = lax.all_gather(local_rows, "blk", axis=0, tiled=True)
        source_ids = jnp.arange(group_size, dtype=jnp.int32)[None, :, None]
        chosen = group_table[source_ids * blocks + near_index]
        near_part = jnp.einsum(
            "rmnij,rmnjk->rik", near_tiles, chosen, preferred_element_type=jnp.float32
        )
        everything = lax.all_gather(local_rows, "grp", axis=0, tiled=True)
        far_rows = everything[far_index * blocks + wanted[far_index]]
        far_part = jnp.einsum(
            "rnij,rnjk->rik", far_tiles, far_rows, preferred_element_type=jnp.float32
        )
        product = near_part + far_part
        flat_rows = product.reshape(blocks * tile_size, vec_width)
        local_gram = jnp.dot(
            flat_rows.T,
            flat_rows,
            precision=lax.Precision.HIGHEST,
            preferred_element_type=jnp.float32,
        )
        gram = lax.psum(local_gram, ("grp", "blk")) / total_rows
        factor = jnp.linalg.cholesky(gram)
        identity_matrix = jnp.eye(vec_width, dtype=jnp.float32)
        inverse = lax.linalg.triangular_solve(factor, identity_matrix, left_side=True, lower=True).T
        vectors = jnp.dot(
            flat_rows, inverse, precision=lax.Precision.HIGHEST, preferred_element_type=jnp.float32
        )
        current = vectors.astype(jnp.bfloat16)
    return vectors


def solution(mesh):
    in_specs = (
        P(("grp", "blk"), None, None),
        P(("grp", "blk"), None),
        P(("grp", "blk"), None, None),
        P(("grp", "blk"), None),
        P(("grp", "blk"), None),
        P(("grp", "blk"), None),
    )
    out_specs = P(("grp", "blk"), None)
    return jax.shard_map(
        per_device, mesh=mesh, in_specs=in_specs, out_specs=out_specs, check_vma=False
    )
```

profile of v0, /device:TPU:1, one launch (start us, length us, event | category | flops | bytes accessed | tf_op | source)
XLA Modules:
  0.0 777.3 jit_solution(7489281376360508679)
XLA Ops:
  6.5 0.7 all-gather.5.cloned.1.call-update
  7.3 0.7 all-gather.7.cloned.1.call-update
  8.1 0.5 broadcast.166
  8.6 1.3 reduce.10
  10.1 1.4 gather_fusion.1
  11.6 1.3 reduce.11
  12.9 0.1 reshape.117
  13.1 0.1 reshape.129
  13.3 37.1 %all-gather.5.cloned.1.call-done = bf16[32,256,128]{2,1,0:T(8,128)(2,1)} async-done(((bf16[4,256,128]{2,1,0:T(8,128)(2,1)}), bf16[32,256,128]{2,1,0:T(8,128)(2,1)}) %all-gather.5.cloned.1.call-update) | async-done | bytes 2097168 | tf_op jit(solution)/shard_map/all_gather | solution.py:27
  50.4 4.6 gather_fusion
  55.0 58.5 %all-gather.7.cloned.1.call-done = bf16[128,256,128]{2,1,0:T(8,128)(2,1)} async-done(((bf16[4,256,128]{2,1,0:T(8,128)(2,1)}), bf16[128,256,128]{2,1,0:T(8,128)(2,1)}) %all-gather.7.cloned.1.call-update) | async-done | bytes 8388624 | tf_op jit(solution)/shard_map/all_gather | solution.py:33
  113.6 5.4 gather_fusion.2
  118.9 2.7 convolution_bitcast_fusion.1
  121.7 5.2 fusion.31
  126.9 0.8 copy-done.1
  127.7 1.2 convolution_bitcast_fusion.3
  129.0 2.0 copy.32
  131.0 235.3 %all-reduce.3.cloned.1.call-done = f32[128,128]{0,1:T(8,128)} async-done(((f32[128,128]{0,1:T(8,128)}), f32[128,128]{0,1:T(8,128)}) %all-reduce.3.cloned.1.call-update) | async-done | bytes 65552 | tf_op jit(solution)/shard_map/psum | solution.py:46
  366.3 0.8 broadcast_multiply_fusion.1
  367.2 0.1 copy.35
  367.3 0.9 fusion.45
  368.1 11.7 %cholesky.44 = f32[128,128]{1,0:T(8,128)S(1)} custom-call(f32[128,128]{1,0:T(8,128)S(1)} %fusion.45), custom_call_target="Cholesky" | custom-call | tf_op jit(solution)/shard_map/jit(cholesky)/cholesky | solution.py:47
  379.9 0.6 compare_reduce_fusion.1
  380.5 0.7 fusion.40
  381.2 9.8 %custom-call.6 = f32[1,128,128]{1,2,0:T(8,128)S(1)} custom-call(f32[1,128,128]{2,1,0:T(8,128)S(1)} %fusion.40), custom_call_target="InvertDiagBlocksLowerTriangular" | custom-call | tf_op jit(solution)/shard_map/triangular_solve/custom-call.0 | solution.py:49
  391.0 0.3 fusion.38
  391.3 2.3 convolution_convert_fusion
  393.7 0.5 all-gather.11.cloned.1.call-update
  394.2 0.2 all-reduce.5.cloned.1.call-start
  394.5 32.8 %all-gather.9.cloned.1.call-done = bf16[32,256,128]{2,1,0:T(8,128)(2,1)} async-done(((bf16[4,256,128]{2,1,0:T(8,128)(2,1)}), bf16[32,256,128]{2,1,0:T(8,128)(2,1)}) %all-gather.9.cloned.1.call-update) | async-done | bytes 2097168 | tf_op jit(solution)/shard_map/all_gather | solution.py:27
  427.3 4.6 gather_fusion.3
  432.0 58.4 %all-gather.11.cloned.1.call-done = bf16[128,256,128]{2,1,0:T(8,128)(2,1)} async-done(((bf16[4,256,128]{2,1,0:T(8,128)(2,1)}), bf16[128,256,128]{2,1,0:T(8,128)(2,1)}) %all-gather.11.cloned.1.call-update) | async-done | bytes 8388624 | tf_op jit(solution)/shard_map/all_gather | solution.py:33
  490.3 5.4 gather_fusion.4
  495.7 2.7 convolution_bitcast_fusion
  498.4 5.2 fusion.21
  503.7 0.8 copy-done.2
  504.5 1.2 convolution_bitcast_fusion.2
  505.7 2.0 copy.39
  507.7 235.3 %all-reduce.5.cloned.1.call-done = f32[128,128]{0,1:T(8,128)} async-done(((f32[128,128]{0,1:T(8,128)}), f32[128,128]{0,1:T(8,128)}) %all-reduce.5.cloned.1.call-update) | async-done | bytes 65552 | tf_op jit(solution)/shard_map/psum | solution.py:46
  743.1 0.8 broadcast_multiply_fusion
  743.9 0.1 copy.42
  744.0 0.9 fusion.43
  744.9 11.7 %cholesky.55 = f32[128,128]{1,0:T(8,128)S(1)} custom-call(f32[128,128]{1,0:T(8,128)S(1)} %fusion.43), custom_call_target="Cholesky" | custom-call | tf_op jit(solution)/shard_map/jit(cholesky)/cholesky | solution.py:47
  756.6 0.6 compare_reduce_fusion
  757.2 0.7 fusion.41
  757.9 9.8 %custom-call.7 = f32[1,128,128]{1,2,0:T(8,128)S(1)} custom-call(f32[1,128,128]{2,1,0:T(8,128)S(1)} %fusion.41), custom_call_target="InvertDiagBlocksLowerTriangular" | custom-call | tf_op jit(solution)/shard_map/triangular_solve/custom-call.0 | solution.py:49
  767.7 0.3 fusion.36
  768.0 2.4 fusion.46
  (29 shorter events, 0.8 us)
Async XLA Ops:
  6.5 112.4 %copy-start = (bf16[24,256,256]{2,1,0:T(8,128)(2,1)S(1)}, bf16[24,256,256]{2,1,0:T(8,128)(2,1)}, u32[]{:S(2)}) copy-start(bf16[24,256,256]{2,1,0:T(8,128)(2,1)} %param.11) | copy-start | bytes 9437188
  6.5 43.8 %all-gather.5.cloned.1.call-start = ((), (), s32[]{:S(2)}) async-start(), calls=%async_computation | async-start | bytes 2359296 | tf_op jit(solution)/shard_map/all_gather | solution.py:27
  7.3 106.3 %all-gather.7.cloned.1.call-start = ((), (), s32[]{:S(2)}) async-start(), calls=%async_computation.1 | async-start | bytes 8650752 | tf_op jit(solution)/shard_map/all_gather | solution.py:33
  8.0 358.3 %all-reduce.3.cloned.1.call-start = ((), (), s32[]{:S(2)}) async-start(), calls=%async_computation.2 | async-start | bytes 131072 | tf_op jit(solution)/shard_map/psum | solution.py:46
  118.9 2.7 copy-start.4
  126.9 0.8 copy-start.1
  128.9 298.4 %all-gather.9.cloned.1.call-start = ((), (), s32[]{:S(2)}) async-start(), calls=%async_computation.3 | async-start | bytes 2359296 | tf_op jit(solution)/shard_map/all_gather | solution.py:27
  393.6 96.7 %all-gather.11.cloned.1.call-start = ((), (), s32[]{:S(2)}) async-start(), calls=%async_computation.4 | async-start | bytes 8650752 | tf_op jit(solution)/shard_map/all_gather | solution.py:33
  394.2 348.8 %all-reduce.5.cloned.1.call-start = ((), (), s32[]{:S(2)}) async-start(), calls=%async_computation.5 | async-start | bytes 131072 | tf_op jit(solution)/shard_map/psum | solution.py:46
  495.7 2.7 copy-start.3
  503.7 0.8 copy-start.2
Sparse Core Ops, SparseCore 0:
  9.1 41.1 all-gather.4
  52.9 60.5 all-gather.6
  129.1 237.2 all-reduce.2
  393.8 33.4 all-gather.8
  429.7 60.5 all-gather.10
  505.8 237.1 all-reduce.4
where the time goes:
time: 778 us; the launch traced here: 777 us
  waiting for transfers between devices  659 us (85%)
  other arithmetic  51.9 us (7%)
  local copies, waits for them, and re-layouts  28.3 us (4%)
  matrix products  23.6 us (3%)
  between operations  13.7 us (2%)
    psum x2, waiting for transfers between devices, per_device(): gram = lax.psum(local_gram, ('grp', 'blk')) / total_rows  471 us
    all_gather x2, waiting for transfers between devices, per_device(): everything = lax.all_gather(local_rows, 'grp', axis=0, tiled=True)  117 us
    all_gather x2, waiting for transfers between devices, per_device(): group_table = lax.all_gather(local_rows, 'blk', axis=0, tiled=True)  70 us
    another operation x6, other arithmetic, per_device(): factor = jnp.linalg.cholesky(gram)  24.8 us
    another operation x4, other arithmetic, per_device(): lax.linalg.triangular_solve(factor, identity_matrix, left_side=True, lowe...  20.9 us
  transfers between devices with their start and end apart: 6, of which 6 were waited for; matrix products, arithmetic and copies ran while one was open for 2% of the time, Pallas kernels for 0%

commit v1 on v0

v1 whole, which is shorter than its diff:
```python
import functools

import jax
import jax.numpy as jnp
from jax import lax
from jax.experimental import pallas as pl
from jax.experimental.pallas import tpu as pltpu
from jax.sharding import PartitionSpec as P

ITERS = 2
MESH = pl.DeviceIdType.MESH
NX, NY, NC, NZ = 4, 4, 2, 8
NG = NX * NY * NC
LINE = NC * NZ
PLANE = NX * NY


def wait_bytes(ref, sem):
    pltpu.make_async_copy(ref, ref, sem).wait()


def product_kernel(
    near_cols, far_groups, need, cur, tiles_near, tiles_far,
    product, gram_out,
    a_near, a_far, near_buf, far_buf, stage, request, wanted,
    gram, rs_buf, part, plane_buf, total, gathered,
    tile_sem, ring_send, ring_recv, req_send, req_recv, far_send, far_recv,
    ar_send, ar_recv,
):
    g = lax.axis_index("grp")
    z = lax.axis_index("blk")
    core = lax.rem(g, NC)
    xy = g // NC
    x, y = xy // NY, lax.rem(xy, NY)
    blocks = cur.shape[0]
    half = blocks // 2

    load_near = pltpu.make_async_copy(tiles_near, a_near, tile_sem.at[0])
    load_far = pltpu.make_async_copy(tiles_far, a_far, tile_sem.at[1])
    load_near.start()
    load_far.start()

    def group_peer(k):
        dc, dy, dx = lax.rem(k, NC), lax.rem(k // NC, NY), k // (NC * NY)
        px, py, pc = lax.rem(x + dx, NX), lax.rem(y + dy, NY), lax.rem(core + dc, NC)
        return (px * NY + py) * NC + pc

    def line_peer(k):
        pz, pc = lax.rem(z + k // NC, NZ), lax.rem(core + lax.rem(k, NC), NC)
        return xy * NC + pc, pz

    def plane_peer(k):
        px, py = lax.rem(x + k // NY, NX), lax.rem(y + lax.rem(k, NY), NY)
        return (px * NY + py) * NC + core

    barrier = pltpu.get_barrier_semaphore()

    def greet_group(k, carry):
        pl.semaphore_signal(barrier, inc=1, device_id=(group_peer(k), z), device_id_type=MESH)
        return carry

    def greet_line(k, carry):
        pl.semaphore_signal(barrier, inc=1, device_id=line_peer(k), device_id_type=MESH)
        return carry

    lax.fori_loop(1, NG, greet_group, 0)
    lax.fori_loop(NC, LINE, greet_line, 0)

    def fill_request(h, carry):
        request[h] = jnp.full(request.shape[1:], need[0, h], jnp.int32).astype(jnp.float32)
        return carry

    lax.fori_loop(0, NG, fill_request, 0)
    near_buf[z] = cur[...]
    far_buf[g] = cur[0]
    pl.semaphore_wait(barrier, NG - 1 + LINE - NC)

    right, left = lax.rem(z + 1, NZ), lax.rem(z + NZ - 1, NZ)

    def ring(direction, step, part_id):
        owner = lax.rem(z + (step if direction else NZ - step), NZ)
        rows = pl.ds(part_id * half, half)
        src = cur.at[rows] if step == 0 else near_buf.at[owner, rows]
        return pltpu.make_async_remote_copy(
            src_ref=src,
            dst_ref=near_buf.at[owner, rows],
            send_sem=ring_send.at[direction],
            recv_sem=ring_recv.at[direction, step, part_id],
            device_id=(g, left if direction else right),
            device_id_type=MESH,
        )

    def parts(direction, step):
        if step < NZ // 2 - 1:
            return (0, 1) if direction == 0 else (1, 0)
        return (direction,)

    for i in range(2):
        for direction in (0, 1):
            ring(direction, 0, parts(direction, 0)[i]).start()

    def request_copy(k):
        peer = group_peer(k)
        return pltpu.make_async_remote_copy(
            src_ref=request.at[peer],
            dst_ref=wanted.at[g],
            send_sem=req_send,
            recv_sem=req_recv,
            device_id=(peer, z),
            device_id_type=MESH,
        )

    def send_request(k, carry):
        request_copy(k).start()
        return carry

    lax.fori_loop(1, NG, send_request, 0)
    wait_bytes(wanted.at[pl.ds(0, NG - 1)], req_recv)

    def send_far(k, carry):
        peer = group_peer(k)
        choice = wanted[peer][None]
        picked = cur[0].astype(jnp.float32).reshape(-1, 8, 128)
        for b in range(1, blocks):
            other = cur[b].astype(jnp.float32).reshape(-1, 8, 128)
            picked = jnp.where(choice == float(b), other, picked)
        stage[peer] = picked.reshape(stage.shape[1:]).astype(stage.dtype)
        pltpu.make_async_remote_copy(
            src_ref=stage.at[peer],
            dst_ref=far_buf.at[g],
            send_sem=far_send,
            recv_sem=far_recv,
            device_id=(peer, z),
            device_id_type=MESH,
        ).start()
        return carry

    lax.fori_loop(1, NG, send_far, 0)

    for step in range(1, NZ // 2):
        for i in range(2):
            for direction in (0, 1):
                order = parts(direction, step - 1)
                here = order[i]
                ring(direction, step - 1, here).wait_recv()
                if here in parts(direction, step):
                    ring(direction, step, here).start()
    for direction in (0, 1):
        ring(direction, NZ // 2 - 1, direction).wait_recv()

    load_near.wait()
    per_row = a_near.shape[0] // blocks
    per_source = per_row // NZ
    far_row = a_far.shape[0] // blocks
    tile = cur.shape[1]

    def near_rows(r, carry):
        acc = jnp.zeros((tile, cur.shape[2]), jnp.float32)
        for j in range(per_row):
            t = r * per_row + j
            acc += jnp.dot(
                a_near[t], near_buf[j // per_source, near_cols[0, t]],
                preferred_element_type=jnp.float32,
            )
        product[pl.ds(r * tile, tile), :] = acc
        return carry

    lax.fori_loop(0, blocks, near_rows, 0)

    load_far.wait()
    wait_bytes(far_buf.at[pl.ds(0, NG - 1)], far_recv)

    def far_rows(r, carry):
        rows = pl.ds(r * tile, tile)
        acc = product[rows, :]
        for j in range(far_row):
            t = r * far_row + j
            acc += jnp.dot(
                a_far[t], far_buf[far_groups[0, t]], preferred_element_type=jnp.float32
            )
        product[rows, :] = acc
        return carry

    lax.fori_loop(0, blocks, far_rows, 0)

    flat = product[...]
    gram[...] = lax.dot_general(
        flat, flat, (((0,), (0,)), ((), ())),
        precision=lax.Precision.HIGHEST, preferred_element_type=jnp.float32,
    ).reshape(gram.shape)

    q = z * NC + core

    def scatter(k, carry):
        pg, pz = line_peer(k)
        pq = pz * NC + lax.rem(pg, NC)
        pltpu.make_async_remote_copy(
            src_ref=gram.at[pq], dst_ref=rs_buf.at[q],
            send_sem=ar_send.at[0], recv_sem=ar_recv.at[0],
            device_id=(pg, pz), device_id_type=MESH,
        ).start()
        return carry

    lax.fori_loop(1, LINE, scatter, 0)
    rs_buf[q] = gram[q]
    wait_bytes(rs_buf.at[pl.ds(0, LINE - 1)], ar_recv.at[0])
    part[...] = jnp.sum(rs_buf[...], axis=0)
    plane_buf[xy] = part[...]

    def spread(k, carry):
        pltpu.make_async_remote_copy(
            src_ref=part, dst_ref=plane_buf.at[xy],
            send_sem=ar_send.at[1], recv_sem=ar_recv.at[1],
            device_id=(plane_peer(k), z), device_id_type=MESH,
        ).start()
        return carry

    lax.fori_loop(1, PLANE, spread, 0)
    wait_bytes(plane_buf.at[pl.ds(0, PLANE - 1)], ar_recv.at[1])
    total[...] = jnp.sum(plane_buf[...], axis=0)
    gathered[q] = total[...]

    def collect(k, carry):
        pltpu.make_async_remote_copy(
            src_ref=total, dst_ref=gathered.at[q],
            send_sem=ar_send.at[2], recv_sem=ar_recv.at[2],
            device_id=line_peer(k), device_id_type=MESH,
        ).start()
        return carry

    lax.fori_loop(1, LINE, collect, 0)
    wait_bytes(gathered.at[pl.ds(0, LINE - 1)], ar_recv.at[2])
    gram_out[...] = gathered[...].reshape(gram_out.shape)

    sent = NZ // 2 * blocks - half
    for direction in (0, 1):
        wait_bytes(far_buf.at[pl.ds(0, sent)], ring_send.at[direction])
    wait_bytes(request.at[pl.ds(0, NG - 1)], req_send)
    wait_bytes(stage.at[pl.ds(0, NG - 1)], far_send)
    wait_bytes(rs_buf.at[pl.ds(0, LINE - 1)], ar_send.at[0])
    wait_bytes(plane_buf.at[pl.ds(0, PLANE - 1)], ar_send.at[1])
    wait_bytes(gathered.at[pl.ds(0, LINE - 1)], ar_send.at[2])


def product_and_gram(near_cols, far_groups, need, cur, tiles_near, tiles_far):
    blocks, tile, width = cur.shape
    rows = width // LINE
    return pl.pallas_call(
        product_kernel,
        out_shape=(
            jax.ShapeDtypeStruct((blocks * tile, width), jnp.float32),
            jax.ShapeDtypeStruct((width, width), jnp.float32),
        ),
        in_specs=[pl.BlockSpec(memory_space=pltpu.SMEM)] * 3
        + [pl.BlockSpec(memory_space=pltpu.VMEM)]
        + [pl.BlockSpec(memory_space=pl.ANY)] * 2,
        out_specs=(pl.BlockSpec(memory_space=pltpu.VMEM),) * 2,
        scratch_shapes=[
            pltpu.VMEM(tiles_near.shape, tiles_near.dtype),
            pltpu.VMEM(tiles_far.shape, tiles_far.dtype),
            pltpu.VMEM((NZ, blocks, tile, width), cur.dtype),
            pltpu.VMEM((NG, tile, width), cur.dtype),
            pltpu.VMEM((NG, tile, width), cur.dtype),
            pltpu.VMEM((NG, 8, 128), jnp.float32),
            pltpu.VMEM((NG, 8, 128), jnp.float32),
            pltpu.VMEM((LINE, rows, width), jnp.float32),
            pltpu.VMEM((LINE, rows, width), jnp.float32),
            pltpu.VMEM((rows, width), jnp.float32),
            pltpu.VMEM((PLANE, rows, width), jnp.float32),
            pltpu.VMEM((rows, width), jnp.float32),
            pltpu.VMEM((LINE, rows, width), jnp.float32),
            pltpu.SemaphoreType.DMA((2,)),
            pltpu.SemaphoreType.DMA((2,)),
            pltpu.SemaphoreType.DMA((2, NZ // 2, 2)),
            pltpu.SemaphoreType.DMA,
            pltpu.SemaphoreType.DMA,
            pltpu.SemaphoreType.DMA,
            pltpu.SemaphoreType.DMA,
            pltpu.SemaphoreType.DMA((3,)),
            pltpu.SemaphoreType.DMA((3,)),
        ],
        compiler_params=pltpu.CompilerParams(
            collective_id=0, has_side_effects=True, vmem_limit_bytes=40 << 20
        ),
        name="product_and_gram",
    )(near_cols, far_groups, need, cur, tiles_near, tiles_far)


def per_device(tiles_near, near_cols, tiles_far, far_groups, need_blocks, start_vectors):
    tile_size = tiles_near.shape[1]
    rows, vec_width = start_vectors.shape
    blocks = rows // tile_size
    total_rows = rows * lax.axis_size("blk") * lax.axis_size("grp")
    current = start_vectors
    for iteration in range(ITERS):
        local_rows = current.reshape(blocks, tile_size, vec_width)
        flat_rows, gram = product_and_gram(
            near_cols, far_groups, need_blocks, local_rows, tiles_near, tiles_far
        )
        gram = gram / total_rows
        factor = jnp.linalg.cholesky(gram)
        identity_matrix = jnp.eye(vec_width, dtype=jnp.float32)
        inverse = lax.linalg.triangular_solve(factor, identity_matrix, left_side=True, lower=True).T
        vectors = jnp.dot(
            flat_rows, inverse, precision=lax.Precision.HIGHEST, preferred_element_type=jnp.float32
        )
        current = vectors.astype(jnp.bfloat16)
    return vectors


def solution(mesh):
    in_specs = (
        P(("grp", "blk"), None, None),
        P(("grp", "blk"), None),
        P(("grp", "blk"), None, None),
        P(("grp", "blk"), None),
        P(("grp", "blk"), None),
        P(("grp", "blk"), None),
    )
    out_specs = P(("grp", "blk"), None)
    return jax.shard_map(
        per_device, mesh=mesh, in_specs=in_specs, out_specs=out_specs, check_vma=False
    )
```

time: 778 us -> 200 us (0.26)
  waiting for transfers between devices: 659 us -> 0 us
  Pallas kernels: 0 us -> 136 us
  matrix products: 23.6 us -> 4.61 us
  local copies, waits for them, and re-layouts: 28.3 us -> 13.5 us
  between operations: 13.7 us -> 0.21 us
    psum x2 -> x0, waiting for transfers between devices: 471 us -> none  [per_device(): gram = lax.psum(local_gram, ('grp', 'blk')) / total_rows]
    all_gather x4 -> x0, waiting for transfers between devices: 187 us -> none  [the longest x2 117 us: per_device(): everything = lax.all_gather(local_rows, 'grp', axis=0, tiled=True)]
    pallas_call x0 -> x2, Pallas kernels: none -> 136 us  [product_and_gram(): pl.pallas_call(product_kernel, out_shape=(jax.ShapeDtypeStruct((blocks *...]
    gather x6 -> x0, local copies, waits for them, and re-layouts: 21.5 us -> none  [the longest x4 12.2 us: per_device(): far_rows = everything[far_index * blocks + wanted[far_index]]]
    dot_general x6 -> x0, matrix products: 18.3 us -> none  [the longest x2 10.5 us: per_device(): jnp.einsum('rmnij,rmnjk->rik', near_tiles, chosen, preferred_element_type...]
    unnamed x11 -> x26, local copies, waits for them, and re-layouts: 2.1 us -> 13.2 us
  transfers between devices with their start and end apart: 6 -> 0, of which waited for: 6 -> 0; matrix products, arithmetic and copies ran while one was open for 2% -> 0% of each run, Pallas kernels for 0% -> 0%
where the time goes in v1:
time: 200 us
  Pallas kernels  136 us (68%)
  other arithmetic  45.7 us (23%)
  local copies, waits for them, and re-layouts  13.5 us (7%)
  matrix products  4.61 us (2%)
    pallas_call x2, Pallas kernels, product_and_gram(): pl.pallas_call(product_kernel, out_shape=(jax.ShapeDtypeStruct((blocks *...  136 us
    another operation x6, other arithmetic, per_device(): factor = jnp.linalg.cholesky(gram)  24.8 us
    another operation x4, other arithmetic, per_device(): lax.linalg.triangular_solve(factor, identity_matrix, left_side=True, lowe...  20.9 us
    unnamed x26, local copies, waits for them, and re-layouts  13.2 us
    dot_general x2, matrix products, per_device(): jnp.dot(flat_rows, inverse, precision=lax.Precision.HIGHEST, preferred_el...  4.04 us

profile of v1, /device:TPU:1, one launch (start us, length us, event | category | flops | bytes accessed | tf_op | source)
XLA Modules:
  0.0 199.7 jit_solution(16571632075665406697)
XLA Ops:
  0.0 0.0 copy-start.12
  0.0 0.0 copy-start.10
  0.0 0.0 copy-start.8
  0.0 0.0 copy-start
  0.0 3.4 %copy-done = bf16[64,256,256]{2,1,0:T(8,128)(2,1)S(1)} copy-done((bf16[64,256,256]{2,1,0:T(8,128)(2,1)S(1)}, bf16[64,256,256]{2,1,0:T(8,128)(2,1)}, u32[]{:S(2)}) %copy-start) | copy-done | bytes 8388632
  3.4 0.0 copy-start.2
  3.4 1.9 copy-done.2
  5.3 0.0 copy-start.6
  5.3 0.9 copy-done.6
  6.3 0.0 copy-start.7
  6.3 0.7 copy-done.7
  6.9 0.0 copy-start.9
  6.9 0.7 copy-done.9
  7.6 0.0 copy-start.11
  7.6 0.7 copy-done.11
  8.2 0.0 copy-start.3
  8.2 70.7 %product_and_gram.2 = (f32[1024,128]{1,0:T(8,128)S(1)}, f32[128,128]{1,0:T(8,128)S(1)}) custom-call(s32[1,64]{1,0:T(1,128)S(1)} %copy-done.7, s32[1,24]{1,0:T(1,128)S(1)} %copy-done.9, s32[1,32]{1,0:T(1,128)S(1)} %copy-done.11, bf16[4,256,128]{2,1,0:T(8,128)(2,1)S(1)} %bitcast.25, bf16[64,256,256]{2,1,0:T(8,128)(2,1)S(1)} %copy-done, ...), custom_call_target="tpu_custom_call" | custom-call | tf_op jit(solution)/shard_map/product_and_gram/pallas_call | solution.py:248
  78.9 0.0 copy-start.5
  79.0 0.8 copy-done.5
  79.7 0.1 copy.7
  79.8 0.1 copy.8
  80.0 11.7 %cholesky.44 = f32[128,128]{1,0:T(8,128)S(1)} custom-call(f32[128,128]{1,0:T(8,128)S(1)} %fusion.9), custom_call_target="Cholesky" | custom-call | tf_op jit(solution)/shard_map/jit(cholesky)/cholesky | solution.py:301
  91.7 0.7 compare_reduce_fusion.1
  92.4 0.6 fusion.4
  93.0 9.8 %custom-call.6 = f32[1,128,128]{1,2,0:T(8,128)S(1)} custom-call(f32[1,128,128]{2,1,0:T(8,128)S(1)} %fusion.4), custom_call_target="InvertDiagBlocksLowerTriangular" | custom-call | tf_op jit(solution)/shard_map/triangular_solve/custom-call.0 | solution.py:303
  102.8 0.3 fusion.2
  103.1 1.6 convolution_convert_fusion
  104.7 0.0 copy-done.12
  104.8 0.0 copy-done.10
  104.8 0.0 copy-done.8
  104.8 0.0 copy-done.3
  104.8 0.0 copy-start.1
  104.8 3.4 %copy-done.1 = bf16[64,256,256]{2,1,0:T(8,128)(2,1)S(1)} copy-done((bf16[64,256,256]{2,1,0:T(8,128)(2,1)S(1)}, bf16[64,256,256]{2,1,0:T(8,128)(2,1)}, u32[]{:S(2)}) %copy-start.1) | copy-done | bytes 8388632
  108.2 64.9 %product_and_gram.3 = (f32[1024,128]{1,0:T(8,128)S(1)}, f32[128,128]{1,0:T(8,128)S(1)}) custom-call(s32[1,64]{1,0:T(1,128)S(1)} %copy-done.8, s32[1,24]{1,0:T(1,128)S(1)} %copy-done.10, s32[1,32]{1,0:T(1,128)S(1)} %copy-done.12, bf16[4,256,128]{2,1,0:T(8,128)(2,1)S(1)} %bitcast.24, bf16[64,256,256]{2,1,0:T(8,128)(2,1)S(1)} %copy-done.1, ...), custom_call_target="tpu_custom_call" | custom-call | tf_op jit(solution)/shard_map/product_and_gram/pallas_call | solution.py:248
  173.1 0.0 copy-start.4
  173.1 0.8 copy-done.4
  173.9 0.1 copy.9
  174.0 0.1 copy.10
  174.1 11.7 %cholesky.55 = f32[128,128]{1,0:T(8,128)S(1)} custom-call(f32[128,128]{1,0:T(8,128)S(1)} %fusion.7), custom_call_target="Cholesky" | custom-call | tf_op jit(solution)/shard_map/jit(cholesky)/cholesky | solution.py:301
  185.8 0.6 compare_reduce_fusion
  186.5 0.7 fusion.5
  187.2 9.8 %custom-call.7 = f32[1,128,128]{1,2,0:T(8,128)S(1)} custom-call(f32[1,128,128]{2,1,0:T(8,128)S(1)} %fusion.5), custom_call_target="InvertDiagBlocksLowerTriangular" | custom-call | tf_op jit(solution)/shard_map/triangular_solve/custom-call.0 | solution.py:303
  197.0 0.3 fusion
  197.3 2.4 %fusion.10 = f32[1024,128]{1,0:T(8,128)} fusion(f32[1024,128]{1,0:T(8,128)} %copy-done.4, f32[128,128]{1,0:T(8,128)S(1)} %fusion), kind=kOutput, calls=%fused_computation.23 | convolution fusion | flops 201326592 | bytes 1114112 | tf_op jit(solution)/shard_map/dot_general | solution.py:304
  (6 shorter events, 0.1 us)
Async XLA Ops:
  0.0 104.8 %copy-start.12 = (s32[1,32]{1,0:T(1,128)S(1)}, s32[1,32]{1,0:T(1,128)}, u32[]{:S(2)}) copy-start(s32[1,32]{1,0:T(1,128)} %need.3) | copy-start | bytes 388
  0.0 104.8 %copy-start.10 = (s32[1,24]{1,0:T(1,128)S(1)}, s32[1,24]{1,0:T(1,128)}, u32[]{:S(2)}) copy-start(s32[1,24]{1,0:T(1,128)} %far_groups.3) | copy-start | bytes 292
  0.0 104.8 %copy-start.8 = (s32[1,64]{1,0:T(1,128)S(1)}, s32[1,64]{1,0:T(1,128)}, u32[]{:S(2)}) copy-start(s32[1,64]{1,0:T(1,128)} %near_cols.3) | copy-start | bytes 772
  0.0 3.4 %copy-start = (bf16[64,256,256]{2,1,0:T(8,128)(2,1)S(1)}, bf16[64,256,256]{2,1,0:T(8,128)(2,1)}, u32[]{:S(2)}) copy-start(bf16[64,256,256]{2,1,0:T(8,128)(2,1)} %tiles_near.3) | copy-start | bytes 25165828
  3.4 1.9 copy-start.2
  5.3 0.9 copy-start.6
  6.3 0.7 copy-start.7
  6.9 0.7 copy-start.9
  7.6 0.7 copy-start.11
  8.2 96.5 %copy-start.3 = (bf16[24,256,256]{2,1,0:T(8,128)(2,1)S(1)}, bf16[24,256,256]{2,1,0:T(8,128)(2,1)}, u32[]{:S(2)}) copy-start(bf16[24,256,256]{2,1,0:T(8,128)(2,1)} %tiles_far.3) | copy-start | bytes 9437188
  78.9 0.8 copy-start.5
  104.8 3.4 %copy-start.1 = (bf16[64,256,256]{2,1,0:T(8,128)(2,1)S(1)}, bf16[64,256,256]{2,1,0:T(8,128)(2,1)}, u32[]{:S(2)}) copy-start(bf16[64,256,256]{2,1,0:T(8,128)(2,1)} %tiles_near.3) | copy-start | bytes 25165828
  173.1 0.8 copy-start.4

commit v2 on v0

v2 whole, which is shorter than its diff:
```python
import jax
import jax.numpy as jnp
from jax import lax
from jax.experimental import pallas as pl
from jax.experimental.pallas import tpu as pltpu
from jax.sharding import PartitionSpec as P

ITERS = 2
MESH = pl.DeviceIdType.MESH
NX, NY, NC, NZ = 4, 4, 2, 8
NG = NX * NY * NC
LINE = NC * NZ
PLANE = NX * NY
PANEL = 8
STEP_BUFFERS = NZ + 6


def wait_bytes(ref, sem):
    pltpu.make_async_copy(ref, ref, sem).wait()


def inverse_factor(gram, work, out):
    n = gram.shape[0]
    row_id = lax.broadcasted_iota(jnp.int32, (n, n), 0)
    col_id = lax.broadcasted_iota(jnp.int32, (n, n), 1)
    work[:, :n] = gram
    work[:, n:] = (row_id == col_id).astype(jnp.float32)
    lane = lax.broadcasted_iota(jnp.int32, (PANEL, n), 1)
    sub = lax.broadcasted_iota(jnp.int32, (PANEL, 2 * n), 0)

    def panel(p, first):
        start = pl.multiple_of(p * PANEL, PANEL)
        top = work[pl.ds(start, PANEL), :]
        diag = pltpu.roll(top[:, :n], lax.rem(n - start, n), 1)
        a, low, solved = {}, {}, []
        for j in range(PANEL):
            for i in range(j, PANEL):
                a[i, j] = jnp.broadcast_to(diag[i : i + 1, j : j + 1], (PANEL, n))
        for j in range(PANEL):
            scale = lax.rsqrt(a[j, j])
            row = jnp.broadcast_to(top[j : j + 1, :], (PANEL, 2 * n))
            for k in range(j):
                row = row - jnp.concatenate([low[j, k]] * 2, 1) * solved[k]
            solved.append(row * jnp.concatenate([scale] * 2, 1))
            for i in range(j + 1, PANEL):
                low[i, j] = a[i, j] * scale
            for k in range(j + 1, PANEL):
                for i in range(k, PANEL):
                    a[i, k] = a[i, k] - low[i, j] * low[k, j]
        block = solved[0]
        for j in range(1, PANEL):
            block = jnp.where(sub == j, solved[j], block)
        out[pl.ds(start, PANEL), :] = block[:, n:]
        left = jnp.where(lane >= start + PANEL, block[:, :n], 0.0)
        columns = left.T[first:].reshape((n - first) // PANEL, PANEL, PANEL)
        rows = pl.ds(first, n - first)
        rest = work[rows, :].reshape((n - first) // PANEL, PANEL, 2 * n)
        for j in range(PANEL):
            rest = rest - columns[:, :, j : j + 1] * solved[j][None]
        work[rows, :] = rest.reshape(n - first, 2 * n)

    def first_half(p, carry):
        panel(p, 0)
        return carry

    def second_half(p, carry):
        panel(p, n // 2)
        return carry

    steps = n // PANEL
    lax.fori_loop(0, steps // 2, first_half, 0)
    lax.fori_loop(steps // 2, steps, second_half, 0)


def iteration_kernel(*refs):
    (near_cols, far_groups, need, start, tiles_near, tiles_far, vectors_out,
     a_near, a_far, stage, request, wanted, product, gram, work, inverse) = refs[:16]
    refs = refs[16:]
    per_step = [refs[i * STEP_BUFFERS : (i + 1) * STEP_BUFFERS] for i in range(ITERS)]
    (tile_sem, ring_send, ring_recv, req_send, req_recv, far_send, far_recv,
     ar_send, ar_recv) = refs[ITERS * STEP_BUFFERS :]

    g = lax.axis_index("grp")
    z = lax.axis_index("blk")
    core = lax.rem(g, NC)
    xy = g // NC
    x, y = xy // NY, lax.rem(xy, NY)
    blocks, tile, width = start.shape
    half = blocks // 2
    rows_each = width // LINE
    q = z * NC + core

    load_near = pltpu.make_async_copy(tiles_near, a_near, tile_sem.at[0])
    load_far = pltpu.make_async_copy(tiles_far, a_far, tile_sem.at[1])
    load_near.start()
    load_far.start()

    def group_peer(k):
        dc, dy, dx = lax.rem(k, NC), lax.rem(k // NC, NY), k // (NC * NY)
        px, py, pc = lax.rem(x + dx, NX), lax.rem(y + dy, NY), lax.rem(core + dc, NC)
        return (px * NY + py) * NC + pc

    def line_peer(k):
        pz, pc = lax.rem(z + k // NC, NZ), lax.rem(core + lax.rem(k, NC), NC)
        return xy * NC + pc, pz

    def plane_peer(k):
        px, py = lax.rem(x + k // NY, NX), lax.rem(y + lax.rem(k, NY), NY)
        return (px * NY + py) * NC + core

    barrier = pltpu.get_barrier_semaphore()

    def greet_group(k, carry):
        pl.semaphore_signal(barrier, inc=1, device_id=(group_peer(k), z), device_id_type=MESH)
        return carry

    def greet_line(k, carry):
        pl.semaphore_signal(barrier, inc=1, device_id=line_peer(k), device_id_type=MESH)
        return carry

    lax.fori_loop(1, NG, greet_group, 0)
    lax.fori_loop(NC, LINE, greet_line, 0)

    def fill_request(h, carry):
        request[h] = jnp.full(request.shape[1:], need[0, h], jnp.int32).astype(jnp.float32)
        return carry

    lax.fori_loop(0, NG, fill_request, 0)
    per_step[0][0][...] = start[...]
    pl.semaphore_wait(barrier, NG - 1 + LINE - NC)

    right, left = lax.rem(z + 1, NZ), lax.rem(z + NZ - 1, NZ)
    last = NZ // 2 - 1

    def parts(direction, step):
        if step < last:
            return (0, 1) if direction == 0 else (1, 0)
        return (direction,)

    def send_request(k, carry):
        peer = group_peer(k)
        pltpu.make_async_remote_copy(
            src_ref=request.at[peer], dst_ref=wanted.at[g],
            send_sem=req_send, recv_sem=req_recv,
            device_id=(peer, z), device_id_type=MESH,
        ).start()
        return carry

    near_row = a_near.shape[0] // blocks
    per_source = near_row // NZ
    far_row = a_far.shape[0] // blocks

    for it in range(ITERS):
        own, away = per_step[it][0], per_step[it][1 : NZ]
        far_buf, rs_buf, part, plane_buf, total, gathered = per_step[it][NZ:]

        def slot(direction, step):
            return away[2 * last] if step == last else away[2 * step + direction]

        def ring(direction, step, part_id):
            rows = pl.ds(part_id * half, half)
            src = own if step == 0 else slot(direction, step - 1)
            return pltpu.make_async_remote_copy(
                src_ref=src.at[rows],
                dst_ref=slot(direction, step).at[rows],
                send_sem=ring_send.at[direction],
                recv_sem=ring_recv.at[it, direction, step, part_id],
                device_id=(g, left if direction else right),
                device_id_type=MESH,
            )

        for i in range(2):
            for direction in (0, 1):
                ring(direction, 0, parts(direction, 0)[i]).start()

        if it == 0:
            lax.fori_loop(1, NG, send_request, 0)
        far_buf[g] = own[0]
        if it == 0:
            wait_bytes(wanted.at[pl.ds(0, NG - 1)], req_recv)

        def send_far(k, carry):
            peer = group_peer(k)
            choice = wanted[peer][None]
            picked = own[0].astype(jnp.float32).reshape(-1, 8, 128)
            for b in range(1, blocks):
                other = own[b].astype(jnp.float32).reshape(-1, 8, 128)
                picked = jnp.where(choice == float(b), other, picked)
            stage[peer] = picked.reshape(stage.shape[1:]).astype(stage.dtype)
            pltpu.make_async_remote_copy(
                src_ref=stage.at[peer], dst_ref=far_buf.at[g],
                send_sem=far_send, recv_sem=far_recv.at[it],
                device_id=(peer, z), device_id_type=MESH,
            ).start()
            return carry

        lax.fori_loop(1, NG, send_far, 0)

        def near_part(shard, source, first):
            def one_row(r, carry):
                rows = pl.ds(pl.multiple_of(r * tile, tile), tile)
                acc = None if first else product[rows, :]
                for n in range(per_source):
                    t = r * near_row + source * per_source + n
                    term = jnp.dot(
                        a_near[t], shard[near_cols[0, t]], preferred_element_type=jnp.float32
                    )
                    acc = term if acc is None else acc + term
                product[rows, :] = acc
                return carry

            lax.fori_loop(0, blocks, one_row, 0)

        if it == 0:
            load_near.wait()
            load_far.wait()
        near_part(own, z, True)
        for step in range(NZ // 2):
            for i in range(2):
                for direction in (0, 1):
                    if i < len(parts(direction, step)):
                        here = parts(direction, step)[i]
                        ring(direction, step, here).wait_recv()
                        if step < last and here in parts(direction, step + 1):
                            ring(direction, step + 1, here).start()
            if step < last:
                near_part(slot(0, step), lax.rem(z + NZ - 1 - step, NZ), False)
                near_part(slot(1, step), lax.rem(z + 1 + step, NZ), False)
            else:
                near_part(slot(0, step), lax.rem(z + NZ // 2, NZ), False)

        wait_bytes(far_buf.at[pl.ds(0, NG - 1)], far_recv.at[it])

        def far_rows(r, carry):
            rows = pl.ds(pl.multiple_of(r * tile, tile), tile)
            acc = product[rows, :]
            for j in range(far_row):
                t = r * far_row + j
                acc += jnp.dot(
                    a_far[t], far_buf[far_groups[0, t]], preferred_element_type=jnp.float32
                )
            product[rows, :] = acc
            return carry

        lax.fori_loop(0, blocks, far_rows, 0)

        flat = product[...]
        gram[...] = lax.dot_general(
            flat, flat, (((0,), (0,)), ((), ())),
            precision=lax.Precision.HIGHEST, preferred_element_type=jnp.float32,
        ).reshape(gram.shape)

        def scatter(k, carry):
            pg, pz = line_peer(k)
            pltpu.make_async_remote_copy(
                src_ref=gram.at[pz * NC + lax.rem(pg, NC)], dst_ref=rs_buf.at[q],
                send_sem=ar_send.at[0], recv_sem=ar_recv.at[it, 0],
                device_id=(pg, pz), device_id_type=MESH,
            ).start()
            return carry

        lax.fori_loop(1, LINE, scatter, 0)
        rs_buf[q] = gram[q]
        wait_bytes(rs_buf.at[pl.ds(0, LINE - 1)], ar_recv.at[it, 0])
        part[...] = jnp.sum(rs_buf[...], axis=0)
        plane_buf[xy] = part[...]

        def spread(k, carry):
            pltpu.make_async_remote_copy(
                src_ref=part, dst_ref=plane_buf.at[xy],
                send_sem=ar_send.at[1], recv_sem=ar_recv.at[it, 1],
                device_id=(plane_peer(k), z), device_id_type=MESH,
            ).start()
            return carry

        lax.fori_loop(1, PLANE, spread, 0)
        wait_bytes(plane_buf.at[pl.ds(0, PLANE - 1)], ar_recv.at[it, 1])
        total[...] = jnp.sum(plane_buf[...], axis=0)
        gathered[q] = total[...]

        def collect(k, carry):
            pltpu.make_async_remote_copy(
                src_ref=total, dst_ref=gathered.at[q],
                send_sem=ar_send.at[2], recv_sem=ar_recv.at[it, 2],
                device_id=line_peer(k), device_id_type=MESH,
            ).start()
            return carry

        lax.fori_loop(1, LINE, collect, 0)
        wait_bytes(gathered.at[pl.ds(0, LINE - 1)], ar_recv.at[it, 2])

        sent = (last + 1) * blocks - half
        for direction in (0, 1):
            wait_bytes(far_buf.at[pl.ds(0, sent)], ring_send.at[direction])
        if it == 0:
            wait_bytes(request.at[pl.ds(0, NG - 1)], req_send)
        wait_bytes(stage.at[pl.ds(0, NG - 1)], far_send)
        wait_bytes(rs_buf.at[pl.ds(0, LINE - 1)], ar_send.at[0])
        wait_bytes(plane_buf.at[pl.ds(0, PLANE - 1)], ar_send.at[1])
        wait_bytes(gathered.at[pl.ds(0, LINE - 1)], ar_send.at[2])

        total_rows = float(blocks * tile * NG * NZ)
        inverse_factor(gathered[...].reshape(width, width) / total_rows, work, inverse)

        def make_vectors(r, carry):
            rows = pl.ds(pl.multiple_of(r * tile, tile), tile)
            block = lax.dot_general(
                product[rows, :], inverse[...], (((1,), (1,)), ((), ())),
                precision=lax.Precision.HIGHEST, preferred_element_type=jnp.float32,
            )
            if it == ITERS - 1:
                vectors_out[rows, :] = block
            else:
                per_step[it + 1][0][r] = block.astype(start.dtype)
            return carry

        lax.fori_loop(0, blocks, make_vectors, 0)


def iterate(near_cols, far_groups, need, start, tiles_near, tiles_far):
    blocks, tile, width = start.shape
    rows = width // LINE
    step_buffers = (
        [pltpu.VMEM((blocks, tile, width), start.dtype)] * NZ
        + [
            pltpu.VMEM((NG, tile, width), start.dtype),
            pltpu.VMEM((LINE, rows, width), jnp.float32),
            pltpu.VMEM((rows, width), jnp.float32),
            pltpu.VMEM((PLANE, rows, width), jnp.float32),
            pltpu.VMEM((rows, width), jnp.float32),
            pltpu.VMEM((LINE, rows, width), jnp.float32),
        ]
    )
    assert len(step_buffers) == STEP_BUFFERS
    return pl.pallas_call(
        iteration_kernel,
        out_shape=jax.ShapeDtypeStruct((blocks * tile, width), jnp.float32),
        in_specs=[pl.BlockSpec(memory_space=pltpu.SMEM)] * 3
        + [pl.BlockSpec(memory_space=pltpu.VMEM)]
        + [pl.BlockSpec(memory_space=pltpu.HBM)] * 2,
        out_specs=pl.BlockSpec(memory_space=pltpu.VMEM),
        scratch_shapes=[
            pltpu.VMEM(tiles_near.shape, tiles_near.dtype),
            pltpu.VMEM(tiles_far.shape, tiles_far.dtype),
            pltpu.VMEM((NG, tile, width), start.dtype),
            pltpu.VMEM((NG, 8, 128), jnp.float32),
            pltpu.VMEM((NG, 8, 128), jnp.float32),
            pltpu.VMEM((blocks * tile, width), jnp.float32),
            pltpu.VMEM((LINE, rows, width), jnp.float32),
            pltpu.VMEM((width, 2 * width), jnp.float32),
            pltpu.VMEM((width, width), jnp.float32),
        ]
        + step_buffers * ITERS
        + [
            pltpu.SemaphoreType.DMA((2,)),
            pltpu.SemaphoreType.DMA((2,)),
            pltpu.SemaphoreType.DMA((ITERS, 2, NZ // 2, 2)),
            pltpu.SemaphoreType.DMA,
            pltpu.SemaphoreType.DMA,
            pltpu.SemaphoreType.DMA,
            pltpu.SemaphoreType.DMA((ITERS,)),
            pltpu.SemaphoreType.DMA((3,)),
            pltpu.SemaphoreType.DMA((ITERS, 3)),
        ],
        compiler_params=pltpu.CompilerParams(
            collective_id=0, has_side_effects=True, vmem_limit_bytes=48 << 20
        ),
        name="iterate",
    )(near_cols, far_groups, need, start, tiles_near, tiles_far)


def per_device(tiles_near, near_cols, tiles_far, far_groups, need_blocks, start_vectors):
    tile_size = tiles_near.shape[1]
    rows, vec_width = start_vectors.shape
    start = start_vectors.reshape(rows // tile_size, tile_size, vec_width)
    return iterate(near_cols, far_groups, need_blocks, start, tiles_near, tiles_far)


def solution(mesh):
    in_specs = (
        P(("grp", "blk"), None, None),
        P(("grp", "blk"), None),
        P(("grp", "blk"), None, None),
        P(("grp", "blk"), None),
        P(("grp", "blk"), None),
        P(("grp", "blk"), None),
    )
    out_specs = P(("grp", "blk"), None)
    return jax.shard_map(
        per_device, mesh=mesh, in_specs=in_specs, out_specs=out_specs, check_vma=False
    )
```

time: 778 us -> 146 us (0.19)
  waiting for transfers between devices: 659 us -> 0 us
  Pallas kernels: 0 us -> 141 us
  other arithmetic: 51.9 us -> 0 us
  matrix products: 23.6 us -> 0 us
  local copies, waits for them, and re-layouts: 28.3 us -> 5.6 us
  between operations: 13.7 us -> 0.01 us
    psum x2 -> x0, waiting for transfers between devices: 471 us -> none  [per_device(): gram = lax.psum(local_gram, ('grp', 'blk')) / total_rows]
    all_gather x4 -> x0, waiting for transfers between devices: 187 us -> none  [the longest x2 117 us: per_device(): everything = lax.all_gather(local_rows, 'grp', axis=0, tiled=True)]
    pallas_call x0 -> x1, Pallas kernels: none -> 141 us  [iterate(): pl.pallas_call(iteration_kernel, out_shape=jax.ShapeDtypeStruct((blocks *...]
    another operation x10 -> x0, other arithmetic: 45.7 us -> none  [the longest x6 24.8 us: per_device(): factor = jnp.linalg.cholesky(gram)]
    dot_general x8 -> x0, matrix products: 23.1 us -> none  [the longest x2 10.5 us: per_device(): jnp.einsum('rmnij,rmnjk->rik', near_tiles, chosen, preferred_element_type...]
    gather x6 -> x0, local copies, waits for them, and re-layouts: 21.5 us -> none  [the longest x4 12.2 us: per_device(): far_rows = everything[far_index * blocks + wanted[far_index]]]
  transfers between devices with their start and end apart: 6 -> 0, of which waited for: 6 -> 0; matrix products, arithmetic and copies ran while one was open for 2% -> 0% of each run, Pallas kernels for 0% -> 0%
where the time goes in v2:
time: 146 us
  Pallas kernels  141 us (97%)
  local copies, waits for them, and re-layouts  5.6 us (4%)
    pallas_call x1, Pallas kernels, iterate(): pl.pallas_call(iteration_kernel, out_shape=jax.ShapeDtypeStruct((blocks *...  141 us
    unnamed x11, local copies, waits for them, and re-layouts  5.6 us

profile of v2, /device:TPU:1, one launch (start us, length us, event | category | flops | bytes accessed | tf_op | source)
XLA Modules:
  0.0 146.1 jit_solution(4860927060245587598)
XLA Ops:
  0.0 0.0 copy-start
  0.0 1.9 %copy-done = bf16[24,256,256]{2,1,0:T(8,128)(2,1)S(1)} copy-done((bf16[24,256,256]{2,1,0:T(8,128)(2,1)S(1)}, bf16[24,256,256]{2,1,0:T(8,128)(2,1)}, u32[]{:S(2)}) %copy-start) | copy-done | bytes 3145752
  1.9 0.0 copy-start.1
  1.9 0.9 copy-done.1
  2.8 0.0 copy-start.2
  2.8 0.7 copy-done.2
  3.5 0.0 copy-start.3
  3.5 0.7 copy-done.3
  4.2 0.0 copy-start.4
  4.2 0.7 copy-done.4
  4.8 140.5 %iterate.1 = f32[1024,128]{1,0:T(8,128)S(1)} custom-call(s32[1,64]{1,0:T(1,128)S(1)} %copy-done.2, s32[1,24]{1,0:T(1,128)S(1)} %copy-done.3, s32[1,32]{1,0:T(1,128)S(1)} %copy-done.4, bf16[4,256,128]{2,1,0:T(8,128)(2,1)S(1)} %bitcast.1, bf16[64,256,256]{2,1,0:T(8,128)(2,1)} %refs_4_.1, bf16[24,256,256]{2,1,0:T(8,128)(2,1)S(1)} %copy-done), custom_call_target="tpu_custom_call" | custom-call | tf_op jit(solution)/shard_map/iterate/pallas_call | solution.py:335
  145.3 0.8 copy.8
Async XLA Ops:
  0.0 1.9 %copy-start = (bf16[24,256,256]{2,1,0:T(8,128)(2,1)S(1)}, bf16[24,256,256]{2,1,0:T(8,128)(2,1)}, u32[]{:S(2)}) copy-start(bf16[24,256,256]{2,1,0:T(8,128)(2,1)} %refs_5_.1) | copy-start | bytes 9437188
  1.9 0.9 copy-start.1
  2.8 0.7 copy-start.2
  3.5 0.7 copy-start.3
  4.2 0.7 copy-start.4

commit v3 on v2

--- a/solution.py
+++ b/solution.py
@@ -11,12 +11,21 @@
 NG = NX * NY * NC
 LINE = NC * NZ
 PLANE = NX * NY
-PANEL = 8
-STEP_BUFFERS = NZ + 6
+PANEL = 16
+SIDE = NX
+STEP_BUFFERS = NZ + SIDE - 1 + 6
+FAR_IN = SIDE * (NC * SIDE - 1)
 
 
 def wait_bytes(ref, sem):
     pltpu.make_async_copy(ref, ref, sem).wait()
+
+
+def split(value):
+    high = value.astype(jnp.bfloat16)
+    rest = value - high.astype(jnp.float32)
+    middle = rest.astype(jnp.bfloat16)
+    return high, middle, (rest - middle.astype(jnp.float32)).astype(jnp.bfloat16)
 
 
 def inverse_factor(gram, work, out):
@@ -25,51 +34,49 @@
     col_id = lax.broadcasted_iota(jnp.int32, (n, n), 1)
     work[:, :n] = gram
     work[:, n:] = (row_id == col_id).astype(jnp.float32)
-    lane = lax.broadcasted_iota(jnp.int32, (PANEL, n), 1)
-    sub = lax.broadcasted_iota(jnp.int32, (PANEL, 2 * n), 0)
-
-    def panel(p, first):
+    sub = lax.broadcasted_iota(jnp.int32, (8, 2 * n), 0)
+
+    def wide(value):
+        return jnp.concatenate([value] * 2, 1)
+
+    def panel(p, carry):
         start = pl.multiple_of(p * PANEL, PANEL)
-        top = work[pl.ds(start, PANEL), :]
+        rows = pl.ds(start, PANEL)
+        top = work[rows, :]
         diag = pltpu.roll(top[:, :n], lax.rem(n - start, n), 1)
-        a, low, solved = {}, {}, []
+        a, low, scale, solved = {}, {}, [], []
         for j in range(PANEL):
             for i in range(j, PANEL):
-                a[i, j] = jnp.broadcast_to(diag[i : i + 1, j : j + 1], (PANEL, n))
+                a[i, j] = jnp.broadcast_to(diag[i : i + 1, j : j + 1], (8, n))
         for j in range(PANEL):
-            scale = lax.rsqrt(a[j, j])
-            row = jnp.broadcast_to(top[j : j + 1, :], (PANEL, 2 * n))
-            for k in range(j):
-                row = row - jnp.concatenate([low[j, k]] * 2, 1) * solved[k]
-            solved.append(row * jnp.concatenate([scale] * 2, 1))
+            scale.append(lax.rsqrt(a[j, j]))
             for i in range(j + 1, PANEL):
-                low[i, j] = a[i, j] * scale
+                low[i, j] = a[i, j] * scale[j]
             for k in range(j + 1, PANEL):
                 for i in range(k, PANEL):
                     a[i, k] = a[i, k] - low[i, j] * low[k, j]
-        block = solved[0]
-        for j in range(1, PANEL):
-            block = jnp.where(sub == j, solved[j], block)
-        out[pl.ds(start, PANEL), :] = block[:, n:]
-        left = jnp.where(lane >= start + PANEL, block[:, :n], 0.0)
-        columns = left.T[first:].reshape((n - first) // PANEL, PANEL, PANEL)
-        rows = pl.ds(first, n - first)
-        rest = work[rows, :].reshape((n - first) // PANEL, PANEL, 2 * n)
         for j in range(PANEL):
-            rest = rest - columns[:, :, j : j + 1] * solved[j][None]
-        work[rows, :] = rest.reshape(n - first, 2 * n)
-
-    def first_half(p, carry):
-        panel(p, 0)
+            row = jnp.broadcast_to(top[j : j + 1, :], (8, 2 * n))
+            for k in range(j):
+                row = row - wide(low[j, k]) * solved[k]
+            solved.append(row * wide(scale[j]))
+        pieces = []
+        for b in range(0, PANEL, 8):
+            piece = solved[b]
+            for j in range(1, 8):
+                piece = jnp.where(sub == j, solved[b + j], piece)
+            pieces.append(piece)
+        block = jnp.concatenate(pieces, 0)
+        out[rows, :] = block[:, n:]
+        high, middle, small = split(block)
+        left = jnp.concatenate([v[:, :n] for v in (high, high, middle, high, small, middle)], 0)
+        right = jnp.concatenate([high, middle, high, small, high, middle], 0)
+        work[...] = work[...] - lax.dot_general(
+            left, right, (((0,), (0,)), ((), ())), preferred_element_type=jnp.float32
+        )
         return carry
 
-    def second_half(p, carry):
-        panel(p, n // 2)
-        return carry
-
-    steps = n // PANEL
-    lax.fori_loop(0, steps // 2, first_half, 0)
-    lax.fori_loop(steps // 2, steps, second_half, 0)
+    lax.fori_loop(0, n // PANEL, panel, 0)
 
 
 def iteration_kernel(*refs):
@@ -77,7 +84,7 @@
      a_near, a_far, stage, request, wanted, product, gram, work, inverse) = refs[:16]
     refs = refs[16:]
     per_step = [refs[i * STEP_BUFFERS : (i + 1) * STEP_BUFFERS] for i in range(ITERS)]
-    (tile_sem, ring_send, ring_recv, req_send, req_recv, far_send, far_recv,
+    (tile_sem, ring_send, ring_recv, req_send, req_recv, share_send, share_recv, far_send, far_recv,
      ar_send, ar_recv) = refs[ITERS * STEP_BUFFERS :]
 
     g = lax.axis_index("grp")
@@ -100,6 +107,17 @@
         px, py, pc = lax.rem(x + dx, NX), lax.rem(y + dy, NY), lax.rem(core + dc, NC)
         return (px * NY + py) * NC + pc
 
+    def group_at(first, second, which):
+        px = first + which * (second - first)
+        py = second + which * (first - second)
+        return px * NY + py
+
+    axis_a = x + core * (y - x)
+    axis_b = y + core * (x - y)
+
+    def same_core(first, second):
+        return group_at(first, second, core) * NC + core
+
     def line_peer(k):
         pz, pc = lax.rem(z + k // NC, NZ), lax.rem(core + lax.rem(k, NC), NC)
         return xy * NC + pc, pz
@@ -121,11 +139,15 @@
     lax.fori_loop(1, NG, greet_group, 0)
     lax.fori_loop(NC, LINE, greet_line, 0)
 
-    def fill_request(h, carry):
-        request[h] = jnp.full(request.shape[1:], need[0, h], jnp.int32).astype(jnp.float32)
+    def fill_request(k, carry):
+        t, b, a = k // (SIDE * SIDE), lax.rem(k // SIDE, SIDE), lax.rem(k, SIDE)
+        source = group_at(a, b, t) * NC + t
+        value = jnp.full(request.shape[3:], need[0, source], jnp.int32).astype(jnp.float32)
+        request[t, b, a] = value
         return carry
 
     lax.fori_loop(0, NG, fill_request, 0)
+    wanted[axis_b * NC + core] = request[core, axis_b]
     per_step[0][0][...] = start[...]
     pl.semaphore_wait(barrier, NG - 1 + LINE - NC)
 
@@ -138,11 +160,14 @@
         return (direction,)
 
     def send_request(k, carry):
-        peer = group_peer(k)
+        t = lax.rem(core + k // SIDE, NC)
+        mine_a, mine_b = x + t * (y - x), y + t * (x - y)
+        b = lax.rem(mine_b + lax.rem(k, SIDE), SIDE)
+        relay = group_at(mine_a, b, t) * NC + t
         pltpu.make_async_remote_copy(
-            src_ref=request.at[peer], dst_ref=wanted.at[g],
+            src_ref=request.at[t, b], dst_ref=wanted.at[mine_b * NC + core],
             send_sem=req_send, recv_sem=req_recv,
-            device_id=(peer, z), device_id_type=MESH,
+            device_id=(relay, z), device_id_type=MESH,
         ).start()
         return carry
 
@@ -152,7 +177,8 @@
 
     for it in range(ITERS):
         own, away = per_step[it][0], per_step[it][1 : NZ]
-        far_buf, rs_buf, part, plane_buf, total, gathered = per_step[it][NZ:]
+        relay_buf = per_step[it][NZ : NZ + SIDE - 1]
+        far_buf, rs_buf, part, plane_buf, total, gathered = per_step[it][NZ + SIDE - 1 :]
 
         def slot(direction, step):
             return away[2 * last] if step == last else away[2 * step + direction]
@@ -174,27 +200,48 @@
                 ring(direction, 0, parts(direction, 0)[i]).start()
 
         if it == 0:
-            lax.fori_loop(1, NG, send_request, 0)
-        far_buf[g] = own[0]
+            lax.fori_loop(1, 2 * SIDE, send_request, 0)
+
+        def share(k):
+            return pltpu.make_async_remote_copy(
+                src_ref=own, dst_ref=relay_buf[SIDE - k - 1],
+                send_sem=share_send, recv_sem=share_recv.at[it, SIDE - k - 1],
+                device_id=(same_core(lax.rem(axis_a + k, SIDE), axis_b), z), device_id_type=MESH,
+            )
+
+        for k in (1, 3, 2):
+            share(k).start()
         if it == 0:
-            wait_bytes(wanted.at[pl.ds(0, NG - 1)], req_recv)
-
-        def send_far(k, carry):
-            peer = group_peer(k)
-            choice = wanted[peer][None]
-            picked = own[0].astype(jnp.float32).reshape(-1, 8, 128)
+            wait_bytes(wanted.at[pl.ds(0, NC * SIDE - 1)], req_recv)
+
+        def choose(shard, ask):
+            choice = ask[None]
+            picked = shard[0].astype(jnp.float32).reshape(-1, 8, 128)
             for b in range(1, blocks):
-                other = own[b].astype(jnp.float32).reshape(-1, 8, 128)
+                other = shard[b].astype(jnp.float32).reshape(-1, 8, 128)
                 picked = jnp.where(choice == float(b), other, picked)
-            stage[peer] = picked.reshape(stage.shape[1:]).astype(stage.dtype)
-            pltpu.make_async_remote_copy(
-                src_ref=stage.at[peer], dst_ref=far_buf.at[g],
-                send_sem=far_send, recv_sem=far_recv.at[it],
-                device_id=(peer, z), device_id_type=MESH,
-            ).start()
-            return carry
-
-        lax.fori_loop(1, NG, send_far, 0)
+            return picked.reshape(tile, width).astype(start.dtype)
+
+        def pass_on(away_by):
+            shard = own if away_by == 0 else relay_buf[away_by - 1]
+            a = lax.rem(axis_a + away_by, SIDE)
+            source = same_core(a, axis_b)
+
+            def send_one(m, carry):
+                b, c = lax.rem(axis_b + m // NC, SIDE), lax.rem(core + lax.rem(m, NC), NC)
+                spot = away_by * (NC * SIDE - 1) + m - 1
+                stage[spot] = choose(shard, wanted[b * NC + c, a])
+                pltpu.make_async_remote_copy(
+                    src_ref=stage.at[spot], dst_ref=far_buf.at[source],
+                    send_sem=far_send, recv_sem=far_recv.at[it],
+                    device_id=(group_at(axis_a, b, core) * NC + c, z), device_id_type=MESH,
+                ).start()
+                return carry
+
+            lax.fori_loop(1, NC * SIDE, send_one, 0)
+            far_buf[source] = choose(shard, wanted[axis_b * NC + core, a])
+
+        pass_on(0)
 
         def near_part(shard, source, first):
             def one_row(r, carry):
@@ -214,7 +261,6 @@
         if it == 0:
             load_near.wait()
             load_far.wait()
-        near_part(own, z, True)
         for step in range(NZ // 2):
             for i in range(2):
                 for direction in (0, 1):
@@ -223,13 +269,18 @@
                         ring(direction, step, here).wait_recv()
                         if step < last and here in parts(direction, step + 1):
                             ring(direction, step + 1, here).start()
+            if step == 0:
+                near_part(own, z, True)
+                for k in (1, 3, 2):
+                    share(SIDE - k).wait_recv()
+                    pass_on(k)
             if step < last:
                 near_part(slot(0, step), lax.rem(z + NZ - 1 - step, NZ), False)
                 near_part(slot(1, step), lax.rem(z + 1 + step, NZ), False)
             else:
                 near_part(slot(0, step), lax.rem(z + NZ // 2, NZ), False)
 
-        wait_bytes(far_buf.at[pl.ds(0, NG - 1)], far_recv.at[it])
+        wait_bytes(far_buf.at[pl.ds(0, FAR_IN)], far_recv.at[it])
 
         def far_rows(r, carry):
             rows = pl.ds(pl.multiple_of(r * tile, tile), tile)
@@ -293,8 +344,9 @@
         for direction in (0, 1):
             wait_bytes(far_buf.at[pl.ds(0, sent)], ring_send.at[direction])
         if it == 0:
-            wait_bytes(request.at[pl.ds(0, NG - 1)], req_send)
-        wait_bytes(stage.at[pl.ds(0, NG - 1)], far_send)
+            wait_bytes(wanted.at[pl.ds(0, NC * SIDE - 1)], req_send)
+        wait_bytes(stage.at[pl.ds(0, FAR_IN)], far_send)
+        wait_bytes(stage.at[pl.ds(0, (SIDE - 1) * blocks)], share_send)
         wait_bytes(rs_buf.at[pl.ds(0, LINE - 1)], ar_send.at[0])
         wait_bytes(plane_buf.at[pl.ds(0, PLANE - 1)], ar_send.at[1])
         wait_bytes(gathered.at[pl.ds(0, LINE - 1)], ar_send.at[2])
@@ -321,7 +373,7 @@
     blocks, tile, width = start.shape
     rows = width // LINE
     step_buffers = (
-        [pltpu.VMEM((blocks, tile, width), start.dtype)] * NZ
+        [pltpu.VMEM((blocks, tile, width), start.dtype)] * (NZ + SIDE - 1)
         + [
             pltpu.VMEM((NG, tile, width), start.dtype),
             pltpu.VMEM((LINE, rows, width), jnp.float32),
@@ -343,8 +395,8 @@
             pltpu.VMEM(tiles_near.shape, tiles_near.dtype),
             pltpu.VMEM(tiles_far.shape, tiles_far.dtype),
             pltpu.VMEM((NG, tile, width), start.dtype),
-            pltpu.VMEM((NG, 8, 128), jnp.float32),
-            pltpu.VMEM((NG, 8, 128), jnp.float32),
+            pltpu.VMEM((NC, SIDE, SIDE, 8, 128), jnp.float32),
+            pltpu.VMEM((NC * SIDE, SIDE, 8, 128), jnp.float32),
             pltpu.VMEM((blocks * tile, width), jnp.float32),
             pltpu.VMEM((LINE, rows, width), jnp.float32),
             pltpu.VMEM((width, 2 * width), jnp.float32),
@@ -358,12 +410,14 @@
             pltpu.SemaphoreType.DMA,
             pltpu.SemaphoreType.DMA,
             pltpu.SemaphoreType.DMA,
+            pltpu.SemaphoreType.DMA((ITERS, SIDE - 1)),
+            pltpu.SemaphoreType.DMA,
             pltpu.SemaphoreType.DMA((ITERS,)),
             pltpu.SemaphoreType.DMA((3,)),
             pltpu.SemaphoreType.DMA((ITERS, 3)),
         ],
         compiler_params=pltpu.CompilerParams(
-            collective_id=0, has_side_effects=True, vmem_limit_bytes=48 << 20
+            collective_id=0, has_side_effects=True, vmem_limit_bytes=60 << 20
         ),
         name="iterate",
     )(near_cols, far_groups, need, start, tiles_near, tiles_far)

time: 146 us -> 113 us (0.77)
  Pallas kernels: 141 us -> 111 us
  local copies, waits for them, and re-layouts: 5.6 us -> 1.87 us
    pallas_call x1, Pallas kernels: 141 us -> 111 us  [iterate(): pl.pallas_call(iteration_kernel, out_shape=jax.ShapeDtypeStruct((blocks *...]
    unnamed x11 -> x1, local copies, waits for them, and re-layouts: 5.6 us -> 1.87 us
where the time goes in v3:
time: 113 us
  Pallas kernels  111 us (98%)
  local copies, waits for them, and re-layouts  1.87 us (2%)
    pallas_call x1, Pallas kernels, iterate(): pl.pallas_call(iteration_kernel, out_shape=jax.ShapeDtypeStruct((blocks *...  111 us

profile of v3, /device:TPU:1, one launch (start us, length us, event | category | flops | bytes accessed | tf_op | source)
XLA Modules:
  0.0 113.0 jit_solution(3603619673617663433)
XLA Ops:
  0.0 111.1 %iterate.1 = f32[1024,128]{1,0:T(8,128)} custom-call(s32[1,64]{1,0:T(1,128)} %refs_0_.1, s32[1,24]{1,0:T(1,128)} %refs_1_.1, s32[1,32]{1,0:T(1,128)} %refs_2_.1, bf16[4,256,128]{2,1,0:T(8,128)(2,1)} %bitcast.1, bf16[64,256,256]{2,1,0:T(8,128)(2,1)} %refs_4_.1, bf16[24,256,256]{2,1,0:T(8,128)(2,1)} %refs_5_.1), custom_call_target="tpu_custom_call" | custom-call | tf_op jit(solution)/shard_map/iterate/pallas_call | solution.py:387
  111.2 1.9 %copy.8 = f32[1024,128]{1,0:T(8,128)} copy(f32[1024,128]{1,0:T(8,128)} %iterate.1) | data formatting | bytes 1048576

commit v4 on v0

v4 whole, which is shorter than its diff:
```python
import functools

import jax
import jax.numpy as jnp
from jax import lax
from jax.experimental import pallas as pl
from jax.experimental.pallas import tpu as pltpu
from jax.sharding import PartitionSpec as P

ITERS = 2
MESH = pl.DeviceIdType.MESH
NX, NY, NC, NZ = 4, 4, 2, 8
NG = NX * NY * NC
LINE = NC * NZ
PLANE = NX * NY
PANEL = 16
SIDE = NX
FAR_IN = SIDE * (NC * SIDE - 1)


def wait_bytes(ref, sem):
    pltpu.make_async_copy(ref, ref, sem).wait()


def split(value):
    high = value.astype(jnp.bfloat16)
    rest = value - high.astype(jnp.float32)
    middle = rest.astype(jnp.bfloat16)
    return high, middle, (rest - middle.astype(jnp.float32)).astype(jnp.bfloat16)


def start_factor(gram, work):
    n = gram.shape[0]
    row_id = lax.broadcasted_iota(jnp.int32, (n, n), 0)
    col_id = lax.broadcasted_iota(jnp.int32, (n, n), 1)
    work[:, :n] = gram
    work[:, n:] = (row_id == col_id).astype(jnp.float32)


def factor_panels(work, out, first, last):
    n = out.shape[0]
    sub = lax.broadcasted_iota(jnp.int32, (8, 2 * n), 0)

    def wide(value):
        return jnp.concatenate([value] * 2, 1)

    def panel(p, carry):
        start = pl.multiple_of(p * PANEL, PANEL)
        rows = pl.ds(start, PANEL)
        top = work[rows, :]
        diag = pltpu.roll(top[:, :n], lax.rem(n - start, n), 1)
        a, low, scale, solved = {}, {}, [], []
        for j in range(PANEL):
            for i in range(j, PANEL):
                a[i, j] = jnp.broadcast_to(diag[i : i + 1, j : j + 1], (8, n))
        for j in range(PANEL):
            scale.append(lax.rsqrt(a[j, j]))
            for i in range(j + 1, PANEL):
                low[i, j] = a[i, j] * scale[j]
            for k in range(j + 1, PANEL):
                for i in range(k, PANEL):
                    a[i, k] = a[i, k] - low[i, j] * low[k, j]
        for j in range(PANEL):
            row = jnp.broadcast_to(top[j : j + 1, :], (8, 2 * n))
            for k in range(j):
                row = row - wide(low[j, k]) * solved[k]
            solved.append(row * wide(scale[j]))
        pieces = []
        for b in range(0, PANEL, 8):
            piece = solved[b]
            for j in range(1, 8):
                piece = jnp.where(sub == j, solved[b + j], piece)
            pieces.append(piece)
        block = jnp.concatenate(pieces, 0)
        out[rows, :] = block[:, n:]
        high, middle, small = split(block)
        left = jnp.concatenate([v[:, :n] for v in (high, high, middle, high, small, middle)], 0)
        right = jnp.concatenate([high, middle, high, small, high, middle], 0)
        work[...] = work[...] - lax.dot_general(
            left, right, (((0,), (0,)), ((), ())), preferred_element_type=jnp.float32
        )
        return carry

    lax.fori_loop(first, last, panel, 0)


def iteration_kernel(names, *refs):
    ref = dict(zip(names, refs))
    near_cols, far_groups, need, start = ref["near_cols"], ref["far_groups"], ref["need"], ref["start"]
    a_near, a_far, request, wanted = ref["a_near"], ref["a_far"], ref["request"], ref["wanted"]
    product, early, work, inverse = ref["product"], ref["early"], ref["work"], ref["inverse"]
    gram = ref["gram"]

    g = lax.axis_index("grp")
    z = lax.axis_index("blk")
    core = lax.rem(g, NC)
    xy = g // NC
    x, y = xy // NY, lax.rem(xy, NY)
    blocks, tile, width = start.shape
    q = z * NC + core
    low_half = lax.broadcasted_iota(jnp.int32, (tile, width), 1) < width // 2
    half_id = lax.broadcasted_iota(jnp.int32, (tile, width), 1) // (width // 2)

    load_near = pltpu.make_async_copy(ref["tiles_near"], a_near, ref["tile_sem"].at[0])
    load_far = pltpu.make_async_copy(ref["tiles_far"], a_far, ref["tile_sem"].at[1])
    load_near.start()
    load_far.start()

    def group_at(first, second, which):
        px = first + which * (second - first)
        py = second + which * (first - second)
        return px * NY + py

    axis_a = x + core * (y - x)
    axis_b = y + core * (x - y)

    def same_core(first, second):
        return group_at(first, second, core) * NC + core

    def group_peer(k):
        dc, dy, dx = lax.rem(k, NC), lax.rem(k // NC, NY), k // (NC * NY)
        px, py, pc = lax.rem(x + dx, NX), lax.rem(y + dy, NY), lax.rem(core + dc, NC)
        return (px * NY + py) * NC + pc

    def line_peer(k):
        pz, pc = lax.rem(z + k // NC, NZ), lax.rem(core + lax.rem(k, NC), NC)
        return xy * NC + pc, pz

    def plane_peer(k):
        px, py = lax.rem(x + k // NY, NX), lax.rem(y + lax.rem(k, NY), NY)
        return (px * NY + py) * NC + core

    def loop(first, last, body):
        def step(k, carry):
            body(k)
            return carry

        lax.fori_loop(first, last, step, 0)

    def block_rows(r):
        return pl.ds(pl.multiple_of(r * tile, tile), tile)

    barrier = pltpu.get_barrier_semaphore()

    def greet_group(k):
        pl.semaphore_signal(barrier, inc=1, device_id=(group_peer(k), z), device_id_type=MESH)

    def greet_line(k):
        pl.semaphore_signal(barrier, inc=1, device_id=line_peer(k), device_id_type=MESH)

    loop(1, NG, greet_group)
    loop(NC, LINE, greet_line)

    def fill_request(k):
        t, b, a = k // (SIDE * SIDE), lax.rem(k // SIDE, SIDE), lax.rem(k, SIDE)
        source = group_at(a, b, t) * NC + t
        value = jnp.full(request.shape[3:], need[0, source], jnp.int32).astype(jnp.float32)
        request[t, b, a] = value

    loop(0, NG, fill_request)
    wanted[axis_b * NC + core] = request[core, axis_b]
    ref["own0"][...] = start[...]
    pl.semaphore_wait(barrier, NG - 1 + LINE - NC)

    right, left = lax.rem(z + 1, NZ), lax.rem(z + NZ - 1, NZ)
    last = NZ // 2 - 1
    seven = wanted.at[pl.ds(0, NC * SIDE - 1)]

    def send_request(k):
        t = lax.rem(core + k // SIDE, NC)
        mine_a, mine_b = x + t * (y - x), y + t * (x - y)
        b = lax.rem(mine_b + lax.rem(k, SIDE), SIDE)
        relay = group_at(mine_a, b, t) * NC + t
        pltpu.make_async_remote_copy(
            src_ref=request.at[t, b], dst_ref=wanted.at[mine_b * NC + core],
            send_sem=ref["req_sem"].at[0], recv_sem=ref["req_sem"].at[1],
            device_id=(relay, z), device_id_type=MESH,
        ).start()

    near_row = a_near.shape[0] // blocks
    per_source = near_row // NZ
    far_row = a_far.shape[0] // blocks

    def parts(direction, step):
        if step < last:
            return (0, 1) if direction == 0 else (1, 0)
        return (direction,)

    class Round:
        def __init__(self, index):
            self.index, self.packed = index, index == 2
            self.own = ref["own%d" % index]
            self.away = [ref["away%d_%d" % (index, i)] for i in range(NZ - 1)]
            self.shared = ref["rows2"] if self.packed else self.own
            self.relay = [ref["relay%d_%d" % (index, i)] for i in range(SIDE - 1)]
            self.far = ref["far%d" % index]
            self.stage = ref["stage2" if self.packed else "stage"]
            self.half = self.own.shape[0] // 2

        def slot(self, direction, step):
            return self.away[2 * last] if step == last else self.away[2 * step + direction]

        def ring(self, direction, step, part):
            rows = pl.ds(part * self.half, self.half)
            src = self.own if step == 0 else self.slot(direction, step - 1)
            return pltpu.make_async_remote_copy(
                src_ref=src.at[rows], dst_ref=self.slot(direction, step).at[rows],
                send_sem=ref["ring_send"].at[self.index, direction],
                recv_sem=ref["ring_recv"].at[self.index, direction, step, part],
                device_id=(g, left if direction else right), device_id_type=MESH,
            )

        def share(self, k):
            return pltpu.make_async_remote_copy(
                src_ref=self.shared, dst_ref=self.relay[SIDE - k - 1],
                send_sem=ref["share_send"].at[self.index],
                recv_sem=ref["share_recv"].at[self.index, SIDE - k - 1],
                device_id=(same_core(lax.rem(axis_a + k, SIDE), axis_b), z), device_id_type=MESH,
            )

        def begin(self):
            for i in range(2):
                for direction in (0, 1):
                    self.ring(direction, 0, parts(direction, 0)[i]).start()
            for k in (1, 3, 2):
                self.share(k).start()

        def choose(self, shard, ask):
            choice = ask[None]
            picked = shard[0].astype(jnp.float32).reshape(-1, 8, 128)
            for b in range(1, blocks):
                other = shard[b].astype(jnp.float32).reshape(-1, 8, 128)
                picked = jnp.where(choice == float(b), other, picked)
            return picked.reshape(self.far.shape[1:]).astype(start.dtype)

        def pass_on(self, away_by):
            if away_by:
                self.share(SIDE - away_by).wait_recv()
            shard = self.relay[away_by - 1] if away_by else self.shared
            a = lax.rem(axis_a + away_by, SIDE)
            source = same_core(a, axis_b)

            def send_one(m):
                b, c = lax.rem(axis_b + m // NC, SIDE), lax.rem(core + lax.rem(m, NC), NC)
                spot = away_by * (NC * SIDE - 1) + m - 1
                self.stage[spot] = self.choose(shard, wanted[b * NC + c, a])
                pltpu.make_async_remote_copy(
                    src_ref=self.stage.at[spot], dst_ref=self.far.at[source],
                    send_sem=ref["far_send"].at[self.index],
                    recv_sem=ref["far_recv"].at[self.index],
                    device_id=(group_at(axis_a, b, core) * NC + c, z), device_id_type=MESH,
                ).start()

            loop(1, NC * SIDE, send_one)
            self.far[source] = self.choose(shard, wanted[axis_b * NC + core, a])

        def forward(self, step, i):
            for direction in (0, 1):
                if i < len(parts(direction, step)):
                    here = parts(direction, step)[i]
                    self.ring(direction, step, here).wait_recv()
                    if step < last and here in parts(direction, step + 1):
                        self.ring(direction, step + 1, here).start()

        def near(self, shard, source, total, first):
            def one_row(r):
                acc = None if first else total[block_rows(r), :]
                for n in range(per_source):
                    t = r * near_row + source * per_source + n
                    col = near_cols[0, t]
                    if self.packed:
                        pair = shard[lax.shift_right_logical(col, 1)]
                        term = jnp.dot(a_near[t], pair, preferred_element_type=jnp.float32)
                        term = jnp.where(half_id == jnp.bitwise_and(col, 1), term, 0.0)
                    else:
                        term = jnp.dot(
                            a_near[t], shard[col], preferred_element_type=jnp.float32
                        )
                    acc = term if acc is None else acc + term
                total[block_rows(r), :] = acc

            loop(0, blocks, one_row)

        def near_own(self, total):
            self.near(self.own, z, total, True)

        def near_step(self, step, total):
            self.near(self.slot(0, step), lax.rem(z + NZ - 1 - step, NZ), total, False)
            if step < last:
                self.near(self.slot(1, step), lax.rem(z + 1 + step, NZ), total, False)

        def far_all(self, total):
            wait_bytes(self.far.at[pl.ds(0, FAR_IN)], ref["far_recv"].at[self.index])
            middle = tile // 2

            def one_row(r):
                acc = total[block_rows(r), :]
                for j in range(far_row):
                    t = r * far_row + j
                    block = self.far[far_groups[0, t]]
                    if self.packed:
                        upper = jnp.dot(
                            a_far[t, :, :middle], block, preferred_element_type=jnp.float32
                        )
                        lower = jnp.dot(
                            a_far[t, :, middle:], block, preferred_element_type=jnp.float32
                        )
                        acc += jnp.where(low_half, upper, lower)
                    else:
                        acc += jnp.dot(a_far[t], block, preferred_element_type=jnp.float32)
                total[block_rows(r), :] = acc

            loop(0, blocks, one_row)

        def finish(self):
            sent = (last + 1) * blocks - blocks // 2
            for direction in (0, 1):
                wait_bytes(
                    self.far.at[pl.ds(0, sent)], ref["ring_send"].at[self.index, direction]
                )
            wait_bytes(self.stage.at[pl.ds(0, FAR_IN)], ref["far_send"].at[self.index])
            wait_bytes(
                self.stage.at[pl.ds(0, (SIDE - 1) * blocks)], ref["share_send"].at[self.index]
            )

    class GramSum:
        def __init__(self, it):
            self.it = it
            self.bufs = [ref["%s%d" % (n, it)] for n in ("rs", "part", "plane", "total", "gathered")]

        def send(self, phase, src, dst, device):
            pltpu.make_async_remote_copy(
                src_ref=src, dst_ref=dst,
                send_sem=ref["ar_send"].at[self.it, phase],
                recv_sem=ref["ar_recv"].at[self.it, phase],
                device_id=device, device_id_type=MESH,
            ).start()

        def scatter(self):
            rs = self.bufs[0]
            flat = product[...]
            gram[...] = lax.dot_general(
                flat, flat, (((0,), (0,)), ((), ())),
                precision=lax.Precision.HIGHEST, preferred_element_type=jnp.float32,
            ).reshape(gram.shape)

            def one(k):
                pg, pz = line_peer(k)
                self.send(0, gram.at[pz * NC + lax.rem(pg, NC)], rs.at[q], (pg, pz))

            loop(1, LINE, one)
            rs[q] = gram[q]

        def spread(self):
            rs, part, plane = self.bufs[:3]
            wait_bytes(rs.at[pl.ds(0, LINE - 1)], ref["ar_recv"].at[self.it, 0])
            part[...] = jnp.sum(rs[...], axis=0)
            plane[xy] = part[...]
            loop(1, PLANE, lambda k: self.send(1, part, plane.at[xy], (plane_peer(k), z)))

        def collect(self):
            plane, total, gathered = self.bufs[2:]
            wait_bytes(plane.at[pl.ds(0, PLANE - 1)], ref["ar_recv"].at[self.it, 1])
            total[...] = jnp.sum(plane[...], axis=0)
            gathered[q] = total[...]
            loop(1, LINE, lambda k: self.send(2, total, gathered.at[q], line_peer(k)))

        def result(self):
            gathered = self.bufs[4]
            wait_bytes(gathered.at[pl.ds(0, LINE - 1)], ref["ar_recv"].at[self.it, 2])
            return gathered[...].reshape(width, width) / float(blocks * tile * NG * NZ)

        def finish(self):
            rs, _, plane, _, gathered = self.bufs
            wait_bytes(rs.at[pl.ds(0, LINE - 1)], ref["ar_send"].at[self.it, 0])
            wait_bytes(plane.at[pl.ds(0, PLANE - 1)], ref["ar_send"].at[self.it, 1])
            wait_bytes(gathered.at[pl.ds(0, LINE - 1)], ref["ar_send"].at[self.it, 2])

    panels = width // PANEL
    to_vectors = (((1,), (1,)), ((), ()))

    def times_inverse(value, factor):
        return lax.dot_general(
            value, factor, to_vectors,
            precision=lax.Precision.HIGHEST, preferred_element_type=jnp.float32,
        )

    first = Round(0)
    first.begin()
    loop(1, 2 * SIDE, send_request)
    wait_bytes(seven, ref["req_sem"].at[1])
    first.pass_on(0)
    load_near.wait()
    load_far.wait()
    first.forward(0, 0)
    first.forward(0, 1)
    first.near_own(product)
    for k in (1, 3, 2):
        first.pass_on(k)
    for step in range(last + 1):
        if step:
            first.forward(step, 0)
            first.forward(step, 1)
        first.near_step(step, product)
    first.far_all(product)
    first.finish()
    wait_bytes(seven, ref["req_sem"].at[0])

    ahead, late = Round(1), Round(2)

    def make_early(r):
        rows = product[block_rows(r), :]
        both = jnp.where(low_half, rows, pltpu.roll(rows, width // 2, 1))
        high = both.astype(start.dtype).astype(jnp.float32)
        ahead.own[r] = jnp.where(low_half, high, both - high).astype(start.dtype)

    loop(0, blocks, make_early)
    ahead.begin()
    sums = GramSum(0)
    sums.scatter()
    ahead.pass_on(0)
    sums.spread()
    ahead.forward(0, 0)
    sums.collect()
    ahead.forward(0, 1)
    ahead.pass_on(1)
    ahead.pass_on(3)
    ahead.pass_on(2)
    start_factor(sums.result(), work)
    ahead.forward(1, 0)
    factor_panels(work, inverse, 0, panels // 2)
    ahead.forward(1, 1)
    factor_panels(work, inverse, panels // 2, panels)

    upper = inverse[width // 2 :, :]
    twice = jnp.concatenate([upper, upper], 0)

    def make_late(i):
        even = times_inverse(product[block_rows(2 * i), :], twice)
        odd = times_inverse(product[block_rows(2 * i + 1), :], twice)
        late.own[i] = jnp.where(low_half, even, odd).astype(start.dtype)
        for j, v in enumerate((even, odd)):
            packed = jnp.where(low_half[: tile // 2], v[: tile // 2], v[tile // 2 :])
            late.shared[2 * i + j] = packed.astype(start.dtype)

    loop(0, blocks // 2, make_late)

    late.begin()
    ahead.forward(2, 0)
    late.pass_on(0)
    ahead.near_own(early)
    ahead.forward(2, 1)
    ahead.near_step(0, early)
    late.forward(0, 0)
    late.forward(0, 1)
    late.pass_on(1)
    late.pass_on(3)
    late.pass_on(2)
    ahead.near_step(1, early)
    ahead.forward(3, 0)
    late.forward(1, 0)
    ahead.near_step(2, early)
    late.forward(1, 1)
    ahead.near_step(3, early)
    ahead.far_all(early)
    late.forward(2, 0)
    late.near_own(product)
    late.forward(2, 1)
    late.near_step(0, product)
    late.near_step(1, product)

    def finish_early(r):
        value = early[block_rows(r), :]
        early[block_rows(r), :] = times_inverse(
            value + pltpu.roll(value, width // 2, 1), inverse[...]
        )

    loop(0, blocks, finish_early)
    late.near_step(2, product)
    late.forward(3, 0)
    late.near_step(3, product)
    late.far_all(product)

    def join(r):
        value = product[block_rows(r), :]
        value = value + pltpu.roll(value, width // 2, 1)
        product[block_rows(r), :] = jnp.where(low_half, early[block_rows(r), :], value)

    loop(0, blocks, join)
    sums.finish()
    sums = GramSum(1)
    sums.scatter()
    ahead.finish()
    late.finish()
    sums.spread()
    sums.collect()
    start_factor(sums.result(), work)
    factor_panels(work, inverse, 0, panels)

    def make_vectors(r):
        ref["vectors"][block_rows(r), :] = times_inverse(product[block_rows(r), :], inverse[...])

    loop(0, blocks, make_vectors)
    sums.finish()


def iterate(near_cols, far_groups, need, start, tiles_near, tiles_far):
    blocks, tile, width = start.shape
    rows = width // LINE
    f32, dtype = jnp.float32, start.dtype
    scratch = {
        "a_near": pltpu.VMEM(tiles_near.shape, dtype),
        "a_far": pltpu.VMEM(tiles_far.shape, dtype),
        "request": pltpu.VMEM((NC, SIDE, SIDE, 8, 128), f32),
        "wanted": pltpu.VMEM((NC * SIDE, SIDE, 8, 128), f32),
        "product": pltpu.VMEM((blocks * tile, width), f32),
        "early": pltpu.VMEM((blocks * tile, width), f32),
        "gram": pltpu.VMEM((LINE, rows, width), f32),
        "work": pltpu.VMEM((width, 2 * width), f32),
        "inverse": pltpu.VMEM((width, width), f32),
        "stage": pltpu.VMEM((NG, tile, width), dtype),
        "stage2": pltpu.VMEM((NG, tile // 2, width), dtype),
        "rows2": pltpu.VMEM((blocks, tile // 2, width), dtype),
    }
    for index in range(3):
        shard = (blocks // 2 if index == 2 else blocks, tile, width)
        height = tile // 2 if index == 2 else tile
        scratch["own%d" % index] = pltpu.VMEM(shard, dtype)
        for i in range(NZ - 1):
            scratch["away%d_%d" % (index, i)] = pltpu.VMEM(shard, dtype)
        for i in range(SIDE - 1):
            scratch["relay%d_%d" % (index, i)] = pltpu.VMEM((blocks, height, width), dtype)
        scratch["far%d" % index] = pltpu.VMEM((NG, height, width), dtype)
    for it in range(ITERS):
        scratch["rs%d" % it] = pltpu.VMEM((LINE, rows, width), f32)
        scratch["part%d" % it] = pltpu.VMEM((rows, width), f32)
        scratch["plane%d" % it] = pltpu.VMEM((PLANE, rows, width), f32)
        scratch["total%d" % it] = pltpu.VMEM((rows, width), f32)
        scratch["gathered%d" % it] = pltpu.VMEM((LINE, rows, width), f32)
    dma = pltpu.SemaphoreType.DMA
    scratch["tile_sem"] = dma((2,))
    scratch["req_sem"] = dma((2,))
    scratch["ring_send"] = dma((3, 2))
    scratch["ring_recv"] = dma((3, 2, NZ // 2, 2))
    scratch["share_send"] = dma((3,))
    scratch["share_recv"] = dma((3, SIDE - 1))
    scratch["far_send"] = dma((3,))
    scratch["far_recv"] = dma((3,))
    scratch["ar_send"] = dma((ITERS, 3))
    scratch["ar_recv"] = dma((ITERS, 3))
    operands = ("near_cols", "far_groups", "need", "start", "tiles_near", "tiles_far")
    names = operands + ("vectors",) + tuple(scratch)
    return pl.pallas_call(
        functools.partial(iteration_kernel, names),
        out_shape=jax.ShapeDtypeStruct((blocks * tile, width), jnp.float32),
        in_specs=[pl.BlockSpec(memory_space=pltpu.SMEM)] * 3
        + [pl.BlockSpec(memory_space=pltpu.VMEM)]
        + [pl.BlockSpec(memory_space=pltpu.HBM)] * 2,
        out_specs=pl.BlockSpec(memory_space=pltpu.VMEM),
        scratch_shapes=list(scratch.values()),
        compiler_params=pltpu.CompilerParams(
            collective_id=0, has_side_effects=True, vmem_limit_bytes=60 << 20
        ),
        name="iterate",
    )(near_cols, far_groups, need, start, tiles_near, tiles_far)


def per_device(tiles_near, near_cols, tiles_far, far_groups, need_blocks, start_vectors):
    tile_size = tiles_near.shape[1]
    rows, vec_width = start_vectors.shape
    start = start_vectors.reshape(rows // tile_size, tile_size, vec_width)
    return iterate(near_cols, far_groups, need_blocks, start, tiles_near, tiles_far)


def solution(mesh):
    in_specs = (
        P(("grp", "blk"), None, None),
        P(("grp", "blk"), None),
        P(("grp", "blk"), None, None),
        P(("grp", "blk"), None),
        P(("grp", "blk"), None),
        P(("grp", "blk"), None),
    )
    out_specs = P(("grp", "blk"), None)
    return jax.shard_map(
        per_device, mesh=mesh, in_specs=in_specs, out_specs=out_specs, check_vma=False
    )
```

time: 778 us -> 119 us (0.15)
  waiting for transfers between devices: 659 us -> 0 us
  Pallas kernels: 0 us -> 117 us
  other arithmetic: 51.9 us -> 0 us
  local copies, waits for them, and re-layouts: 28.3 us -> 1.87 us
  matrix products: 23.6 us -> 0 us
  between operations: 13.7 us -> 0.01 us
    psum x2 -> x0, waiting for transfers between devices: 471 us -> none  [per_device(): gram = lax.psum(local_gram, ('grp', 'blk')) / total_rows]
    all_gather x4 -> x0, waiting for transfers between devices: 187 us -> none  [the longest x2 117 us: per_device(): everything = lax.all_gather(local_rows, 'grp', axis=0, tiled=True)]
    pallas_call x0 -> x1, Pallas kernels: none -> 117 us  [iterate(): pl.pallas_call(functools.partial(iteration_kernel, names), out_shape=jax....]
    another operation x10 -> x0, other arithmetic: 45.7 us -> none  [the longest x6 24.8 us: per_device(): factor = jnp.linalg.cholesky(gram)]
    dot_general x8 -> x0, matrix products: 23.1 us -> none  [the longest x2 10.5 us: per_device(): jnp.einsum('rmnij,rmnjk->rik', near_tiles, chosen, preferred_element_type...]
    gather x6 -> x0, local copies, waits for them, and re-layouts: 21.5 us -> none  [the longest x4 12.2 us: per_device(): far_rows = everything[far_index * blocks + wanted[far_index]]]
  transfers between devices with their start and end apart: 6 -> 0, of which waited for: 6 -> 0; matrix products, arithmetic and copies ran while one was open for 2% -> 0% of each run, Pallas kernels for 0% -> 0%
where the time goes in v4:
time: 119 us
  Pallas kernels  117 us (98%)
  local copies, waits for them, and re-layouts  1.87 us (2%)
    pallas_call x1, Pallas kernels, iterate(): pl.pallas_call(functools.partial(iteration_kernel, names), out_shape=jax....  117 us

profile of v4, /device:TPU:1, one launch (start us, length us, event | category | flops | bytes accessed | tf_op | source)
XLA Modules:
  0.0 119.0 jit_solution(8046234741000006857)
XLA Ops:
  0.0 117.2 %iterate.1 = f32[1024,128]{1,0:T(8,128)} custom-call(s32[1,64]{1,0:T(1,128)} %refs_0_.1, s32[1,24]{1,0:T(1,128)} %refs_1_.1, s32[1,32]{1,0:T(1,128)} %refs_2_.1, bf16[4,256,128]{2,1,0:T(8,128)(2,1)} %bitcast.1, bf16[64,256,256]{2,1,0:T(8,128)(2,1)} %refs_4_.1, bf16[24,256,256]{2,1,0:T(8,128)(2,1)} %refs_5_.1), custom_call_target="tpu_custom_call" | custom-call | tf_op jit(solution)/shard_map/iterate/pallas_call | solution.py:553
  117.2 1.9 %copy.8 = f32[1024,128]{1,0:T(8,128)} copy(f32[1024,128]{1,0:T(8,128)} %iterate.1) | data formatting | bytes 1048576

commit v5 on v3

--- a/solution.py
+++ b/solution.py
@@ -102,11 +102,6 @@
     load_near.start()
     load_far.start()
 
-    def group_peer(k):
-        dc, dy, dx = lax.rem(k, NC), lax.rem(k // NC, NY), k // (NC * NY)
-        px, py, pc = lax.rem(x + dx, NX), lax.rem(y + dy, NY), lax.rem(core + dc, NC)
-        return (px * NY + py) * NC + pc
-
     def group_at(first, second, which):
         px = first + which * (second - first)
         py = second + which * (first - second)
@@ -119,25 +114,38 @@
         return group_at(first, second, core) * NC + core
 
     def line_peer(k):
-        pz, pc = lax.rem(z + k // NC, NZ), lax.rem(core + lax.rem(k, NC), NC)
+        pz, pc = lax.rem(z + k // NC, NZ), lax.rem(core + (k % NC), NC)
         return xy * NC + pc, pz
 
     def plane_peer(k):
-        px, py = lax.rem(x + k // NY, NX), lax.rem(y + lax.rem(k, NY), NY)
+        px, py = lax.rem(x + k // NY, NX), lax.rem(y + (k % NY), NY)
         return (px * NY + py) * NC + core
 
+    line_order = sorted(range(1, LINE), key=lambda k: -min(k // NC, NZ - k // NC))
+    plane_order = sorted(
+        range(1, PLANE), key=lambda k: -min(k // NY, NX - k // NY) - min(k % NY, NY - k % NY)
+    )
     barrier = pltpu.get_barrier_semaphore()
 
-    def greet_group(k, carry):
-        pl.semaphore_signal(barrier, inc=1, device_id=(group_peer(k), z), device_id_type=MESH)
-        return carry
+    def greet(group, position):
+        pl.semaphore_signal(barrier, inc=1, device_id=(group, position), device_id_type=MESH)
 
     def greet_line(k, carry):
-        pl.semaphore_signal(barrier, inc=1, device_id=line_peer(k), device_id_type=MESH)
-        return carry
-
-    lax.fori_loop(1, NG, greet_group, 0)
-    lax.fori_loop(NC, LINE, greet_line, 0)
+        greet(*line_peer(k))
+        return carry
+
+    def greet_plane(k, carry):
+        greet(plane_peer(k), z)
+        return carry
+
+    def greet_cross(k, carry):
+        greet(group_at(axis_a, lax.rem(axis_b + k, SIDE), core) * NC + 1 - core, z)
+        greet(group_at(lax.rem(axis_a + k, SIDE), axis_b, core) * NC + 1 - core, z)
+        return carry
+
+    lax.fori_loop(1, LINE, greet_line, 0)
+    lax.fori_loop(1, PLANE, greet_plane, 0)
+    lax.fori_loop(1, SIDE, greet_cross, 0)
 
     def fill_request(k, carry):
         t, b, a = k // (SIDE * SIDE), lax.rem(k // SIDE, SIDE), lax.rem(k, SIDE)
@@ -149,7 +157,7 @@
     lax.fori_loop(0, NG, fill_request, 0)
     wanted[axis_b * NC + core] = request[core, axis_b]
     per_step[0][0][...] = start[...]
-    pl.semaphore_wait(barrier, NG - 1 + LINE - NC)
+    pl.semaphore_wait(barrier, LINE - 1 + PLANE - 1 + 2 * (SIDE - 1))
 
     right, left = lax.rem(z + 1, NZ), lax.rem(z + NZ - 1, NZ)
     last = NZ // 2 - 1
@@ -256,31 +264,7 @@
                 product[rows, :] = acc
                 return carry
 
-            lax.fori_loop(0, blocks, one_row, 0)
-
-        if it == 0:
-            load_near.wait()
-            load_far.wait()
-        for step in range(NZ // 2):
-            for i in range(2):
-                for direction in (0, 1):
-                    if i < len(parts(direction, step)):
-                        here = parts(direction, step)[i]
-                        ring(direction, step, here).wait_recv()
-                        if step < last and here in parts(direction, step + 1):
-                            ring(direction, step + 1, here).start()
-            if step == 0:
-                near_part(own, z, True)
-                for k in (1, 3, 2):
-                    share(SIDE - k).wait_recv()
-                    pass_on(k)
-            if step < last:
-                near_part(slot(0, step), lax.rem(z + NZ - 1 - step, NZ), False)
-                near_part(slot(1, step), lax.rem(z + 1 + step, NZ), False)
-            else:
-                near_part(slot(0, step), lax.rem(z + NZ // 2, NZ), False)
-
-        wait_bytes(far_buf.at[pl.ds(0, FAR_IN)], far_recv.at[it])
+            lax.fori_loop(0, blocks, one_row, 0, unroll=True)
 
         def far_rows(r, carry):
             rows = pl.ds(pl.multiple_of(r * tile, tile), tile)
@@ -293,7 +277,32 @@
             product[rows, :] = acc
             return carry
 
-        lax.fori_loop(0, blocks, far_rows, 0)
+        def forward(step):
+            for i in range(2):
+                for direction in (0, 1):
+                    if i < len(parts(direction, step)):
+                        here = parts(direction, step)[i]
+                        ring(direction, step, here).wait_recv()
+                        if step < last and here in parts(direction, step + 1):
+                            ring(direction, step + 1, here).start()
+
+        if it == 0:
+            load_near.wait()
+            load_far.wait()
+        near_part(own, z, True)
+        forward(0)
+        for k in (1, 3, 2):
+            share(SIDE - k).wait_recv()
+            pass_on(k)
+        for step in range(last):
+            if step:
+                forward(step)
+            near_part(slot(0, step), lax.rem(z + NZ - 1 - step, NZ), False)
+            near_part(slot(1, step), lax.rem(z + 1 + step, NZ), False)
+        wait_bytes(far_buf.at[pl.ds(0, FAR_IN)], far_recv.at[it])
+        lax.fori_loop(0, blocks, far_rows, 0, unroll=True)
+        forward(last)
+        near_part(slot(0, last), lax.rem(z + NZ // 2, NZ), False)
 
         flat = product[...]
         gram[...] = lax.dot_general(
@@ -310,7 +319,8 @@
             ).start()
             return carry
 
-        lax.fori_loop(1, LINE, scatter, 0)
+        for k in line_order:
+            scatter(k, 0)
         rs_buf[q] = gram[q]
         wait_bytes(rs_buf.at[pl.ds(0, LINE - 1)], ar_recv.at[it, 0])
         part[...] = jnp.sum(rs_buf[...], axis=0)
@@ -324,7 +334,8 @@
             ).start()
             return carry
 
-        lax.fori_loop(1, PLANE, spread, 0)
+        for k in plane_order:
+            spread(k, 0)
         wait_bytes(plane_buf.at[pl.ds(0, PLANE - 1)], ar_recv.at[it, 1])
         total[...] = jnp.sum(plane_buf[...], axis=0)
         gathered[q] = total[...]
@@ -337,7 +348,8 @@
             ).start()
             return carry
 
-        lax.fori_loop(1, LINE, collect, 0)
+        for k in line_order:
+            collect(k, 0)
         wait_bytes(gathered.at[pl.ds(0, LINE - 1)], ar_recv.at[it, 2])
 
         sent = (last + 1) * blocks - half

time: 113 us -> 106 us (0.938)
  Pallas kernels: 111 us -> 104 us
    pallas_call x1, Pallas kernels: 111 us -> 104 us  [iterate(): pl.pallas_call(iteration_kernel, out_shape=jax.ShapeDtypeStruct((blocks *...]
where the time goes in v5:
time: 106 us; the launch traced here: 105 us
  Pallas kernels  104 us (98%)
  local copies, waits for them, and re-layouts  1.87 us (2%)
    pallas_call x1, Pallas kernels, iterate(): pl.pallas_call(iteration_kernel, out_shape=jax.ShapeDtypeStruct((blocks *...  104 us

profile of v5, /device:TPU:1, one launch (start us, length us, event | category | flops | bytes accessed | tf_op | source)
XLA Modules:
  0.0 105.5 jit_solution(14321814427971187281)
XLA Ops:
  0.0 103.6 %iterate.1 = f32[1024,128]{1,0:T(8,128)} custom-call(s32[1,64]{1,0:T(1,128)} %refs_0_.1, s32[1,24]{1,0:T(1,128)} %refs_1_.1, s32[1,32]{1,0:T(1,128)} %refs_2_.1, bf16[4,256,128]{2,1,0:T(8,128)(2,1)} %bitcast.1, bf16[64,256,256]{2,1,0:T(8,128)(2,1)} %refs_4_.1, bf16[24,256,256]{2,1,0:T(8,128)(2,1)} %refs_5_.1), custom_call_target="tpu_custom_call" | custom-call | tf_op jit(solution)/shard_map/iterate/pallas_call | solution.py:399
  103.6 1.9 %copy.8 = f32[1024,128]{1,0:T(8,128)} copy(f32[1024,128]{1,0:T(8,128)} %iterate.1) | data formatting | bytes 1048576

commit v6 on v5

--- a/solution.py
+++ b/solution.py
@@ -378,7 +378,7 @@
                 per_step[it + 1][0][r] = block.astype(start.dtype)
             return carry
 
-        lax.fori_loop(0, blocks, make_vectors, 0)
+        lax.fori_loop(0, blocks, make_vectors, 0, unroll=True)
 
 
 def iterate(near_cols, far_groups, need, start, tiles_near, tiles_far):

time: 106 us -> 105 us (level)
  Pallas kernels: 104 us -> 102 us
    pallas_call x1, Pallas kernels: 104 us -> 102 us  [iterate(): pl.pallas_call(iteration_kernel, out_shape=jax.ShapeDtypeStruct((blocks *...]
where the time goes in v6:
time: 105 us; the launch traced here: 104 us
  Pallas kernels  102 us (97%)
  local copies, waits for them, and re-layouts  1.87 us (2%)
    pallas_call x1, Pallas kernels, iterate(): pl.pallas_call(iteration_kernel, out_shape=jax.ShapeDtypeStruct((blocks *...  102 us

profile of v6, /device:TPU:1, one launch (start us, length us, event | category | flops | bytes accessed | tf_op | source)
XLA Modules:
  0.0 104.4 jit_solution(8306235052362472123)
XLA Ops:
  0.0 102.5 %iterate.1 = f32[1024,128]{1,0:T(8,128)} custom-call(s32[1,64]{1,0:T(1,128)} %refs_0_.1, s32[1,24]{1,0:T(1,128)} %refs_1_.1, s32[1,32]{1,0:T(1,128)} %refs_2_.1, bf16[4,256,128]{2,1,0:T(8,128)(2,1)} %bitcast.1, bf16[64,256,256]{2,1,0:T(8,128)(2,1)} %refs_4_.1, bf16[24,256,256]{2,1,0:T(8,128)(2,1)} %refs_5_.1), custom_call_target="tpu_custom_call" | custom-call | tf_op jit(solution)/shard_map/iterate/pallas_call | solution.py:399
  102.5 1.9 %copy.8 = f32[1024,128]{1,0:T(8,128)} copy(f32[1024,128]{1,0:T(8,128)} %iterate.1) | data formatting | bytes 1048576
